TPU v7x, 32 devices: a whole 2x2x4 slice. The times are simulated.
32 devices in a mesh: freq: 4 (over y, x), panel: 8 (over z, core).
Axes of the slice: x: 2, y: 2, z: 4, core: 2. Of those that a mesh axis runs over, the one named last changes fastest.
Arguments:
- fields: bfloat16 [128, 16, 16384], P('freq', None, 'panel'), may hold values from -6 to 6
- quad_index: int32 [16384], P('panel'), may hold values from 0 to 5
- band_width: int32 [128], P('freq'), may hold values from 1 to 64, as said below
Outputs:
- pair_blocks: float32 [128, 16384], P('freq', 'panel')
Inputs may be any that keep to these rules, and one draw needn't show every extreme that they name: `band_width`: some frequency has band width exactly 64.
All inputs are finite; a program needn't handle non-finite values.
Results may differ from a plain program's by a relative error of at most 0.0029.
Values may be sent and summed in bfloat16 or wider, within the bound.
A program may use at most 128 MiB of HBM per device.

v0:
```python
import functools
import math

import jax
import jax.numpy as jnp
from jax import lax
from jax.experimental import pallas as pl
from jax.experimental.pallas import tpu as pltpu
from jax.sharding import PartitionSpec as P

COMP = 16
REACH = 2
LANES = 128
CORES = 2
MESH = pl.DeviceIdType.MESH

QUAD_TABLE = (0.2, 0.45, 0.8, 1.1, 1.6, 2.3)


def shifted(x, axis, by):
    devices = lax.axis_size(axis)
    pairs = [(i, i + by) for i in range(devices) if 0 <= i + by < devices]
    return lax.ppermute(x, axis, pairs)


def plain(fields, quad_index, band_width):
    freq_local = fields.shape[0]
    panel_local = fields.shape[2]
    band = REACH * freq_local
    table = jnp.asarray(QUAD_TABLE, jnp.float32)
    matches = quad_index[None, :] == jnp.arange(6, dtype=jnp.int32)[:, None]
    weight = jnp.sum(jnp.where(matches, table[:, None], jnp.float32(0.0)), 0)
    scaled = (fields.astype(jnp.float32) * weight).astype(jnp.bfloat16)
    own_rows = scaled.reshape(freq_local * COMP, panel_local)
    partners = [fields]
    for distance in range(1, REACH + 1):
        partners.append(shifted(fields, "freq", -distance))
    grams = []
    for partner in partners:
        grams.append(
            lax.dot_general(
                own_rows,
                partner.reshape(freq_local * COMP, panel_local),
                (((1,), (1,)), ((), ())),
                preferred_element_type=jnp.float32,
            )
        )
    stacked = jnp.concatenate(grams, 1).reshape(freq_local, COMP, (REACH + 1) * freq_local, COMP)

    def pick_band(block, row_index):
        return lax.dynamic_slice_in_dim(block, row_index + 1, band, 1)

    picked = jax.vmap(pick_band)(stacked, jnp.arange(freq_local, dtype=jnp.int32))
    picked = picked.transpose(0, 2, 1, 3)
    offsets = jnp.arange(band, dtype=jnp.int32) + 1
    live_mask = offsets[None, :] <= band_width[:, None]
    picked = jnp.where(live_mask[:, :, None, None], picked, jnp.float32(0.0))
    panels_total = panel_local * lax.axis_size("panel")
    terms = picked.reshape(freq_local, band * COMP * COMP) * jnp.float32(
        1.0 / math.sqrt(panels_total)
    )
    return lax.psum_scatter(terms, "panel", scatter_dimension=1, tiled=True)


OWN, XG, DG = 0, 1, 2


def kernel(
    nf, npan, f_hbm, q_ref, bw_ref, out_ref,
    own, scaled, xbuf, ubuf, dbuf, xs, ds, acc, keep, away, cxin, zout, zin, total, give, fwd, fin,
    local_sem, fsend, frecv, csend, crecv, zsend, zrecv, gsend, grecv,
):
    rows, panels = own.shape
    half = panels // 2
    block = rows
    freqs = rows // COMP
    oct_rows = 8 * COMP
    octs = rows // oct_rows
    nz = npan // CORES
    f32, bf16 = jnp.float32, jnp.bfloat16

    f = lax.axis_index("freq")
    p = lax.axis_index("panel")
    z, core = p // CORES, lax.rem(p, CORES)
    odd = lax.rem(f, 2)
    mate = f + 1 - 2 * odd
    has_u = f + 2 < nf
    has_d = f >= 2
    has_x = jnp.logical_or(odd == 1, has_u)
    partner = p + 1 - 2 * core

    def dev(ff, pp):
        return {"freq": ff, "panel": pp}

    load = pltpu.make_async_copy(f_hbm, own, local_sem)
    load.start()

    barrier = pltpu.get_barrier_semaphore()

    def greet(ff, pp):
        pl.semaphore_signal(barrier, inc=1, device_id=dev(ff, pp), device_id_type=MESH)

    greet(mate, p)
    greet(f, partner)
    for zd in range(nz):
        @pl.when(z != zd)
        def _(zd=zd):
            greet(f, zd * CORES + core)

    @pl.when(has_u)
    def _():
        greet(f + 2, p)

    @pl.when(has_d)
    def _():
        greet(f - 2, p)

    count = 1 + nz + jnp.where(has_u, 1, 0) + jnp.where(has_d, 1, 0)
    pl.semaphore_wait(barrier, count)

    def half_at(which):
        return pl.ds(pl.multiple_of(which * half, LANES), half)

    def rows_of(o, n=1):
        return pl.ds(pl.multiple_of(o * oct_rows, oct_rows), n * oct_rows)

    def field_copy(which, dst, slot, ff, o):
        return pltpu.make_async_remote_copy(
            src_ref=f_hbm.at[rows_of(o), half_at(which)], dst_ref=dst.at[rows_of(o), :],
            send_sem=fsend.at[slot, o], recv_sem=frecv.at[slot, o],
            device_id=dev(ff, p), device_id_type=MESH,
        )

    def to_mate(o):
        return field_copy(1 - odd, xbuf, 0, mate, o)

    def to_lower(o):
        return field_copy(0, ubuf, 1, f - 2, o)

    def to_upper(o):
        return field_copy(1, dbuf, 2, f + 2, o)

    for o in range(octs):
        to_mate(octs - 1 - o).start()

        @pl.when(has_d)
        def _(o=o):
            to_lower(o).start()

        @pl.when(has_u)
        def _(o=o):
            to_upper(octs - 1 - o).start()

    def weight_at(where):
        index = q_ref[:, where]
        w = jnp.zeros(index.shape, f32)
        for value, entry in enumerate(QUAD_TABLE):
            w = jnp.where(index == value, jnp.float32(entry), w)
        return w

    def scale(src, dst, where, o, n):
        w = weight_at(where)

        def step(i, carry):
            at = pl.ds(pl.multiple_of(o * oct_rows + i * 32, 32), 32)
            dst[at, :] = (src[at, :].astype(f32) * w).astype(bf16)
            return carry

        lax.fori_loop(0, n * oct_rows // 32, step, 0)

    def gram(left, left_at, lo, n, right, right_at, ro, m, slot, rel):
        tall = 2 if n % 2 == 0 else 1
        first_col = rel * block + ro * oct_rows

        def step(i, carry):
            at = rows_of(lo + i * tall, tall)
            acc[slot, at, first_col:first_col + m * oct_rows] = lax.dot_general(
                left[at, left_at], right[ro * oct_rows:(ro + m) * oct_rows, right_at],
                (((1,), (1,)), ((), ())), preferred_element_type=f32,
            )
            return carry

        if n == tall:
            step(0, 0)
        else:
            lax.fori_loop(0, n // tall, step, 0)

    def clear(slot, tile):
        acc[slot, :, tile * LANES:(tile + 1) * LANES] = jnp.zeros((rows, LANES), f32)

    clear(XG, octs - 1)
    clear(XG, 2 * octs)
    clear(DG, octs - 1)

    @pl.when(odd == 0)
    def _():
        clear(DG, 2 * octs - 1)

    @pl.when(odd == 1)
    def _():
        clear(OWN, octs)
        clear(OWN, 2 * octs - 1)

    @pl.when(jnp.logical_not(has_u))
    def _():
        clear(OWN, 2 * octs)

    def valid(slot, o, pp):
        t = o + pp
        low, high = t >= octs - 1, t <= 2 * octs - 1
        if slot == OWN:
            return jnp.logical_or(
                t <= octs - 1,
                jnp.logical_or(
                    jnp.logical_and(odd == 0, high),
                    jnp.logical_and(has_u, t >= 2 * octs - 1),
                ),
            )
        if slot == XG:
            return jnp.logical_and(has_x, jnp.logical_and(low, high))
        upper = jnp.logical_or(t >= 2 * octs - 1, jnp.logical_and(odd == 1, low))
        return jnp.logical_and(has_d, upper)

    def core_copy(slot, o, pp):
        zd = pp // CORES
        return pltpu.make_async_remote_copy(
            src_ref=away.at[slot, pp, rows_of(o), :], dst_ref=cxin.at[slot, zd, rows_of(o), :],
            send_sem=csend.at[slot, zd, o], recv_sem=crecv.at[slot, zd, o],
            device_id=dev(f, partner), device_id_type=MESH,
        )

    def z_copy(slot, o, zd, source):
        return pltpu.make_async_remote_copy(
            src_ref=zout.at[slot, zd, rows_of(o), :], dst_ref=zin.at[slot, source, rows_of(o), :],
            send_sem=zsend.at[slot, zd, o], recv_sem=zrecv.at[slot, source, o],
            device_id=dev(f, zd * CORES + core), device_id_type=MESH,
        )

    def walk(act, slot, o, t, n, do, dt):
        def step(i, carry):
            oo, tt = o + i * do, t + i * dt
            act(slot, oo, tt - oo, tt)
            return carry

        if n > 0:
            lax.fori_loop(0, n, step, 0)

    def make(slot, o, pp, t):
        lane = pl.multiple_of(t * LANES, LANES)
        for c in range(8):
            at = pl.ds(pl.multiple_of(o * oct_rows + c * COMP, COMP), COMP)
            if c == 7:
                value = acc[slot, at, pl.ds(pl.multiple_of(lane + LANES, LANES), LANES)]
            else:
                pair = acc[slot, at, pl.ds(lane, 2 * LANES)]
                value = pltpu.roll(pair, 2 * LANES - COMP * (c + 1), 1)[:, :LANES]
            keep[slot, pp, at, :] = value
            away[slot, pp, at, :] = value.astype(bf16)

        @pl.when(lax.rem(pp, CORES) != core)
        def _():
            core_copy(slot, o, pp).start()

    def join(slot, o, pp, t):
        @pl.when(lax.rem(pp, CORES) == core)
        def _():
            zd = pp // CORES
            core_copy(slot, o, pp).wait_recv()
            both = keep[slot, pp, rows_of(o), :] + cxin[slot, zd, rows_of(o), :].astype(f32)

            @pl.when(z == zd)
            def _():
                total[slot, rows_of(o), :] = both

            @pl.when(z != zd)
            def _():
                zout[slot, zd, rows_of(o), :] = both.astype(bf16)
                z_copy(slot, o, zd, z).start()

    def both_ways(jobs):
        for act in (make, join):
            for job in jobs:
                if len(job) == 2:
                    @pl.when(job[0])
                    def _(job=job, act=act):
                        for inner in job[1]:
                            walk(act, *inner)
                else:
                    walk(act, *job)

    load.wait()
    everything = pl.ds(0, panels)
    first = pl.ds(0, half)
    second = pl.ds(half, half)
    even_now, odd_now = odd == 0, odd == 1
    scale(own, scaled, everything, 0, octs)
    gram(scaled, everything, 0, octs, own, everything, 0, octs, OWN, 0)
    jobs = [(OWN, 0, t, t + 1, 1, 0) for t in range(octs - 1)]
    jobs.append((odd_now, [(OWN, 0, octs - 1, octs, 1, 0)]))
    both_ways(jobs)

    for i in range(octs):
        x = octs - 1 - i
        last = i == octs - 1
        to_mate(x).wait_recv()
        scale(xbuf, xs, half_at(odd), x, 1)
        jobs = []

        @pl.when(odd_now)
        def _(x=x):
            gram(xs, first, x, 1, own, second, 0, octs, XG, 1)

        jobs.append((odd_now, [(XG, x, octs - 1, octs + 1, 0, 1)]))

        @pl.when(even_now)
        def _(x=x):
            gram(scaled, first, 0, octs, xbuf, first, x, 1, OWN, 1)

        @pl.when(has_u)
        def _(i=i):
            to_lower(i).wait_recv()
            gram(scaled, first, i, octs - i, ubuf, first, i, 1, OWN, 2)

        @pl.when(jnp.logical_and(has_u, even_now))
        def _(i=i, x=x):
            gram(xs, first, x, 1, ubuf, first, 0, i + 1, XG, 1)
            if i:
                gram(xs, first, x + 1, i, ubuf, first, i, 1, XG, 1)

        mixed = [(XG, x, octs - 1, i + 1 + last, 0, 1), (XG, x + 1, octs - 1 + i, i, 1, 0)]
        if last:
            mixed.append((XG, x + 1, 2 * octs - 1, i, 1, 0))
        jobs.append((jnp.logical_and(has_u, even_now), mixed))

        @pl.when(has_d)
        def _(x=x):
            to_upper(x).wait_recv()
            scale(dbuf, ds, second, x, 1)
            gram(ds, first, x, 1, own, second, 0, x + 1, DG, 2)

        @pl.when(jnp.logical_and(has_d, odd_now))
        def _(i=i, x=x):
            gram(ds, first, x, 1, xbuf, first, x, i + 1, DG, 1)
            if i:
                gram(ds, first, x + 1, i, xbuf, first, x, 1, DG, 1)

        mixed = [
            (DG, x, octs + x - last, i + 1 + last, 0, 1),
            (DG, x + 1, octs + x, i, 1, 0),
            (DG, x, 2 * octs, x, 0, 1),
        ]
        if last:
            mixed.append((DG, x + 1, octs - 1, i, 1, 0))
        jobs.append((jnp.logical_and(has_d, odd_now), mixed))
        jobs.append((jnp.logical_and(has_d, even_now), [(DG, x, 2 * octs - 1, x + 1, 0, 1)]))
        own_even = [(OWN, 0, octs + x, octs, 1, 0)]
        if last:
            own_even.append((OWN, 0, octs - 1, octs, 1, 0))
        jobs.append((even_now, own_even))
        if i == 0:
            jobs.append((jnp.logical_and(has_u, odd_now), [(OWN, 0, 2 * octs - 1, octs, 1, 0)]))
        else:
            jobs.append((has_u, [(OWN, i, 2 * octs - 1 + i, octs - i, 1, 0)]))
        both_ways(jobs)

    def forward(slot, ff, o):
        return pltpu.make_async_remote_copy(
            src_ref=give.at[slot, rows_of(o), :], dst_ref=fwd.at[slot, rows_of(o), :],
            send_sem=gsend.at[slot, o], recv_sem=grecv.at[slot, o],
            device_id=dev(ff, p), device_id_type=MESH,
        )

    def settle(slot, target):
        def step(o, carry):
            here = valid(slot, o, p)

            @pl.when(here)
            def _():
                value = total[slot, rows_of(o), :]
                for hop in range(1, nz):
                    source = lax.rem(z + hop, nz)
                    z_copy(slot, o, z, source).wait_recv()
                    value = value + zin[slot, source, rows_of(o), :].astype(f32)
                total[slot, rows_of(o), :] = value
                if target is not None:
                    give[slot, rows_of(o), :] = value.astype(bf16)
                    forward(slot, target, o).start()

            if target is None:
                @pl.when(jnp.logical_not(here))
                def _():
                    total[slot, rows_of(o), :] = jnp.zeros((oct_rows, LANES), f32)

            return carry

        lax.fori_loop(0, octs, step, 0)

    settle(XG, mate)
    settle(DG, f - 2)
    settle(OWN, None)

    def drain(slot):
        def step(i, carry):
            pp, o = i // octs, lax.rem(i, octs)
            zd = pp // CORES

            @pl.when(valid(slot, o, pp))
            def _():
                @pl.when(lax.rem(pp, CORES) != core)
                def _():
                    core_copy(slot, o, pp).wait_send()

                @pl.when(jnp.logical_and(lax.rem(pp, CORES) == core, z != zd))
                def _():
                    z_copy(slot, o, zd, z).wait_send()

            return carry

        lax.fori_loop(0, npan * octs, step, 0)

    for slot in (OWN, XG, DG):
        drain(slot)

    mate_gives = jnp.logical_or(odd == 0, f + 1 < nf)

    def take(slot, giver, comes):
        def step(o, carry):
            @pl.when(comes(o))
            def _():
                forward(slot, giver, o).wait_recv()
                total[OWN, rows_of(o), :] = total[OWN, rows_of(o), :] + fwd[slot, rows_of(o), :].astype(f32)

            return carry

        lax.fori_loop(0, octs, step, 0)

    def from_mate(o):
        t = o + p
        return jnp.logical_and(mate_gives, jnp.logical_and(t >= octs - 1, t <= 2 * octs - 1))

    def from_upper(o):
        t = o + p
        reach = jnp.logical_or(t >= 2 * octs - 1, jnp.logical_and(odd == 1, t >= octs - 1))
        return jnp.logical_and(has_u, reach)

    take(XG, mate, from_mate)
    take(DG, f - 2, from_upper)

    fin[...] = total[OWN]
    eye = lax.broadcasted_iota(jnp.int32, (freqs, freqs), 0) == lax.broadcasted_iota(
        jnp.int32, (freqs, freqs), 1
    )
    width = jnp.sum(
        jnp.where(eye, jnp.broadcast_to(bw_ref[...].astype(f32), (freqs, freqs)), 0.0), 1, keepdims=True
    )
    width = jnp.broadcast_to(width, (freqs, LANES))
    norm = jnp.float32(1.0 / math.sqrt(panels * npan))
    part = lax.broadcasted_iota(jnp.int32, (freqs, LANES), 1) // COMP
    for h in range(COMP // 8):
        values = [fin[pl.ds(h * 8 + a, freqs, stride=COMP), :] for a in range(8)]
        for bit in (1, 2, 4):
            upper = lax.rem(part // bit, 2) == 1
            fresh = list(values)
            for i in range(8):
                if i & bit:
                    continue
                j = i | bit
                fresh[i] = jnp.where(upper, pltpu.roll(values[j], COMP * bit, 1), values[i])
                fresh[j] = jnp.where(upper, values[j], pltpu.roll(values[i], LANES - COMP * bit, 1))
            values = fresh
        for k in range(8):
            offset = (p * 8 + k + 1).astype(f32)
            live = offset <= width
            start = (k * (COMP // 8) + h) * LANES
            out_ref[:, start:start + LANES] = jnp.where(live, values[k] * norm, 0.0)

    def close(o, carry):
        to_mate(o).wait_send()

        @pl.when(has_d)
        def _():
            to_lower(o).wait_send()

        @pl.when(has_u)
        def _():
            to_upper(o).wait_send()

        @pl.when(valid(XG, o, p))
        def _():
            forward(XG, mate, o).wait_send()

        @pl.when(valid(DG, o, p))
        def _():
            forward(DG, f - 2, o).wait_send()

        return carry

    lax.fori_loop(0, octs, close, 0)


def fused(nf, npan, fields, quad_index, band_width):
    freqs, comp, panels = fields.shape
    rows = freqs * comp
    nz = npan // CORES
    half = panels // 2
    octs = freqs // 8
    out_cols = REACH * freqs * comp * comp // npan
    bf16, f32 = jnp.bfloat16, jnp.float32
    dma = pltpu.SemaphoreType.DMA
    vmem = pl.BlockSpec(memory_space=pltpu.VMEM)
    return pl.pallas_call(
        functools.partial(kernel, nf, npan),
        out_shape=jax.ShapeDtypeStruct((freqs, out_cols), f32),
        in_specs=[pl.BlockSpec(memory_space=pl.ANY), vmem, vmem],
        out_specs=vmem,
        scratch_shapes=[
            pltpu.VMEM((rows, panels), bf16),
            pltpu.VMEM((rows, panels), bf16),
            pltpu.VMEM((rows, half), bf16),
            pltpu.VMEM((rows, half), bf16),
            pltpu.VMEM((rows, half), bf16),
            pltpu.VMEM((rows, half), bf16),
            pltpu.VMEM((rows, half), bf16),
            pltpu.VMEM((3, rows, (REACH + 1) * rows), f32),
            pltpu.VMEM((3, npan, rows, LANES), f32),
            pltpu.VMEM((3, npan, rows, LANES), bf16),
            pltpu.VMEM((3, nz, rows, LANES), bf16),
            pltpu.VMEM((3, nz, rows, LANES), bf16),
            pltpu.VMEM((3, nz, rows, LANES), bf16),
            pltpu.VMEM((3, rows, LANES), f32),
            pltpu.VMEM((3, rows, LANES), bf16),
            pltpu.VMEM((3, rows, LANES), bf16),
            pltpu.VMEM((rows, LANES), f32),
            dma,
            dma((3, octs)), dma((3, octs)),
            dma((3, nz, octs)), dma((3, nz, octs)),
            dma((3, nz, octs)), dma((3, nz, octs)),
            dma((3, octs)), dma((3, octs)),
        ],
        compiler_params=pltpu.CompilerParams(
            collective_id=0, has_side_effects=True, vmem_limit_bytes=58 * 1024 * 1024
        ),
    )(fields.reshape(rows, panels), quad_index.reshape(1, panels), band_width.reshape(1, freqs))


def local(nf, npan, fields, quad_index, band_width):
    freqs, comp, panels = fields.shape
    share = REACH * freqs * comp // npan
    fits = nf % 2 == 0 and npan % CORES == 0 and share == LANES and freqs % 8 == 0 and panels % (4 * LANES) == 0
    if not fits:
        return plain(fields, quad_index, band_width)
    return fused(nf, npan, fields, quad_index, band_width)


def solution(mesh):
    placed = (P("freq", None, "panel"), P("panel"), P("freq"))
    return jax.shard_map(
        functools.partial(local, mesh.shape["freq"], mesh.shape["panel"]),
        mesh=mesh, in_specs=placed, out_specs=P("freq", "panel"), check_vma=False,
    )
```

profile of v0, /device:TPU:0, one launch (start us, length us, event | category | flops | bytes accessed | tf_op | source)
XLA Modules:
  0.0 49.5 jit_solution(7391131065126980879)
XLA Ops:
  0.0 47.8 %shard_map.37 = f32[32,2048]{1,0:T(8,128)} custom-call(bf16[512,2048]{1,0:T(8,128)(2,1)} %bitcast.3, s32[1,2048]{1,0:T(1,128)} %bitcast.4, s32[1,32]{1,0:T(1,128)} %bitcast.5), custom_call_target="tpu_custom_call" | custom-call | tf_op jit(solution)/shard_map/pallas_call | solution.py:511
  47.8 1.7 %copy.5 = f32[32,2048]{1,0:T(8,128)} copy(f32[32,2048]{1,0:T(8,128)} %shard_map.37) | data formatting | bytes 524288
where the time goes:
time: 49.7 us; the launch traced here: 49.5 us
  Pallas kernels  47.8 us (96%)
  local copies, waits for them, and re-layouts  1.67 us (3%)
    pallas_call x1, Pallas kernels, fused(): pl.pallas_call(functools.partial(kernel, nf, npan), out_shape=jax.ShapeDt...  47.8 us
    unnamed x1, local copies, waits for them, and re-layouts  1.67 us

commit v1 on v0

--- a/solution.py
+++ b/solution.py
@@ -66,9 +66,9 @@
 
 
 def kernel(
-    nf, npan, f_hbm, q_ref, bw_ref, out_ref,
+    nf, npan, f_hbm, q_hbm, bw_hbm, out_ref,
     own, scaled, xbuf, ubuf, dbuf, xs, ds, acc, keep, away, cxin, zout, zin, total, give, fwd, fin,
-    local_sem, fsend, frecv, csend, crecv, zsend, zrecv, gsend, grecv,
+    q_ref, bw_ref, near, local_sem, fsend, frecv, csend, crecv, zsend, zrecv, gsend, grecv,
 ):
     rows, panels = own.shape
     half = panels // 2
@@ -92,20 +92,23 @@
     def dev(ff, pp):
         return {"freq": ff, "panel": pp}
 
-    load = pltpu.make_async_copy(f_hbm, own, local_sem)
-    load.start()
 
     barrier = pltpu.get_barrier_semaphore()
+    below, above = z > 0, z < nz - 1
 
     def greet(ff, pp):
         pl.semaphore_signal(barrier, inc=1, device_id=dev(ff, pp), device_id_type=MESH)
 
     greet(mate, p)
     greet(f, partner)
-    for zd in range(nz):
-        @pl.when(z != zd)
-        def _(zd=zd):
-            greet(f, zd * CORES + core)
+
+    @pl.when(below)
+    def _():
+        greet(f, p - CORES)
+
+    @pl.when(above)
+    def _():
+        greet(f, p + CORES)
 
     @pl.when(has_u)
     def _():
@@ -115,7 +118,17 @@
     def _():
         greet(f - 2, p)
 
-    count = 1 + nz + jnp.where(has_u, 1, 0) + jnp.where(has_d, 1, 0)
+    loads = [
+        pltpu.make_async_copy(f_hbm, own, local_sem.at[0]),
+        pltpu.make_async_copy(q_hbm, q_ref, local_sem.at[1]),
+        pltpu.make_async_copy(bw_hbm, bw_ref, local_sem.at[2]),
+    ]
+    for load in loads:
+        load.start()
+
+    count = 2
+    for there in (below, above, has_u, has_d):
+        count = count + jnp.where(there, 1, 0)
     pl.semaphore_wait(barrier, count)
 
     def half_at(which):
@@ -150,6 +163,23 @@
         @pl.when(has_u)
         def _(o=o):
             to_upper(octs - 1 - o).start()
+
+    for far in range(1, nz - 1):
+        @pl.when(jnp.logical_and(above, z >= far))
+        def _(far=far):
+            pl.semaphore_signal(near.at[0, far - 1], inc=1, device_id=dev(f, p + CORES), device_id_type=MESH)
+
+        @pl.when(jnp.logical_and(below, z + far < nz))
+        def _(far=far):
+            pl.semaphore_signal(near.at[1, far - 1], inc=1, device_id=dev(f, p - CORES), device_id_type=MESH)
+
+        @pl.when(z > far)
+        def _(far=far):
+            pl.semaphore_wait(near.at[0, far - 1], 1)
+
+        @pl.when(z + 1 + far < nz)
+        def _(far=far):
+            pl.semaphore_wait(near.at[1, far - 1], 1)
 
     def weight_at(where):
         index = q_ref[:, where]
@@ -288,7 +318,8 @@
                 else:
                     walk(act, *job)
 
-    load.wait()
+    for load in loads:
+        load.wait()
     everything = pl.ds(0, panels)
     first = pl.ds(0, half)
     second = pl.ds(half, half)
@@ -511,7 +542,7 @@
     return pl.pallas_call(
         functools.partial(kernel, nf, npan),
         out_shape=jax.ShapeDtypeStruct((freqs, out_cols), f32),
-        in_specs=[pl.BlockSpec(memory_space=pl.ANY), vmem, vmem],
+        in_specs=[pl.BlockSpec(memory_space=pl.ANY)] * 3,
         out_specs=vmem,
         scratch_shapes=[
             pltpu.VMEM((rows, panels), bf16),
@@ -531,7 +562,10 @@
             pltpu.VMEM((3, rows, LANES), bf16),
             pltpu.VMEM((3, rows, LANES), bf16),
             pltpu.VMEM((rows, LANES), f32),
-            dma,
+            pltpu.VMEM((1, panels), jnp.int32),
+            pltpu.VMEM((1, freqs), jnp.int32),
+            pltpu.SemaphoreType.REGULAR((2, max(nz - 2, 1))),
+            dma((3,)),
             dma((3, octs)), dma((3, octs)),
             dma((3, nz, octs)), dma((3, nz, octs)),
             dma((3, nz, octs)), dma((3, nz, octs)),

time: 49.7 us -> 48.8 us (0.982)
  Pallas kernels: 47.8 us -> 46.9 us
    pallas_call x1, Pallas kernels: 47.8 us -> 46.9 us  [fused(): pl.pallas_call(functools.partial(kernel, nf, npan), out_shape=jax.ShapeDt...]
where the time goes in v1:
time: 48.8 us; the launch traced here: 48.6 us
  Pallas kernels  46.9 us (96%)
  local copies, waits for them, and re-layouts  1.67 us (3%)
    pallas_call x1, Pallas kernels, fused(): pl.pallas_call(functools.partial(kernel, nf, npan), out_shape=jax.ShapeDt...  46.9 us
    unnamed x1, local copies, waits for them, and re-layouts  1.67 us

profile of v1, /device:TPU:0, one launch (start us, length us, event | category | flops | bytes accessed | tf_op | source)
XLA Modules:
  0.0 48.6 jit_solution(15914079385889993727)
XLA Ops:
  0.0 46.9 %shard_map.37 = f32[32,2048]{1,0:T(8,128)} custom-call(bf16[512,2048]{1,0:T(8,128)(2,1)} %bitcast.3, s32[1,2048]{1,0:T(1,128)} %bitcast.4, s32[1,32]{1,0:T(1,128)} %bitcast.5), custom_call_target="tpu_custom_call" | custom-call | tf_op jit(solution)/shard_map/pallas_call | solution.py:542
  46.9 1.7 %copy.5 = f32[32,2048]{1,0:T(8,128)} copy(f32[32,2048]{1,0:T(8,128)} %shard_map.37) | data formatting | bytes 524288

commit v2 on v1

--- a/solution.py
+++ b/solution.py
@@ -65,9 +65,79 @@
 OWN, XG, DG = 0, 1, 2
 
 
+def pieces(octs, rising):
+    rows = 8 * COMP
+    found = [(o * rows, rows) for o in range(1, octs)]
+    found = [(rows // 2, rows // 2), (0, rows // 2)] if not rising else []
+    if rising:
+        found = [(o * rows, rows) for o in range(octs - 1)]
+        found += [((octs - 1) * rows, rows // 2), ((octs - 1) * rows + rows // 2, rows // 2)]
+    else:
+        found = [(o * rows, rows) for o in range(octs - 1, 0, -1)] + found
+    return found
+
+
+def arrival(octs, rising):
+    unit = 4 * COMP
+    when = {}
+    for step, (start, rows) in enumerate(pieces(octs, rising)):
+        for u in range(start // unit, (start + rows) // unit):
+            when[u] = step
+    return when
+
+
+def ready(role, octs, x_at, y_at, slot, row, col):
+    block, col = divmod(col, 2 * octs)
+    even, low = role % 2 == 0, role < 2
+    if slot == OWN:
+        if block == 0:
+            return 0
+        if block == 1 and even:
+            return 2 * x_at[col] + 2
+        if block == 2 and low:
+            return 2 * y_at[col] + 3
+    if slot == XG and block == 1:
+        if not even:
+            return 2 * x_at[row] + 2
+        if low:
+            return 2 * max(x_at[row], y_at[col]) + 3
+    if slot == DG and not low:
+        if block == 2:
+            return 2 * y_at[row] + 3
+        if block == 1 and not even:
+            return 2 * max(y_at[row], x_at[col]) + 3
+    return None
+
+
+def plan(role, octs, npan):
+    x_at, y_at = arrival(octs, False), arrival(octs, role < 2)
+    batches, blank = {}, set()
+    for slot in (OWN, XG, DG):
+        for o in range(octs):
+            for pp in range(npan):
+                t = o + pp
+                halves = []
+                for h in range(2):
+                    times = [ready(role, octs, x_at, y_at, slot, 2 * o + h, 2 * t + h + k) for k in range(3)]
+                    halves.append(times)
+                if all(time is None for times in halves for time in times):
+                    continue
+                for h, times in enumerate(halves):
+                    for k, time in enumerate(times):
+                        if time is None:
+                            blank.add((slot, (2 * t + h + k) // 2))
+                due = [max([0] + [time for time in times if time is not None]) for times in halves]
+                if due[0] == due[1]:
+                    batches.setdefault(due[0], []).append((slot, o, 0, 2, pp))
+                else:
+                    for h in range(2):
+                        batches.setdefault(due[h], []).append((slot, o, h, 1, pp))
+    return batches, sorted(blank)
+
+
 def kernel(
     nf, npan, f_hbm, q_hbm, bw_hbm, out_ref,
-    own, scaled, xbuf, ubuf, dbuf, xs, ds, acc, keep, away, cxin, zout, zin, total, give, fwd, fin,
+    own, scaled, xbuf, ybuf, xs, ys, acc, keep, away, cxin, zout, zin, total, give, fwd, fin,
     q_ref, bw_ref, near, local_sem, fsend, frecv, csend, crecv, zsend, zrecv, gsend, grecv,
 ):
     rows, panels = own.shape
@@ -137,32 +207,34 @@
     def rows_of(o, n=1):
         return pl.ds(pl.multiple_of(o * oct_rows, oct_rows), n * oct_rows)
 
-    def field_copy(which, dst, slot, ff, o):
+    def field_copy(which, dst, slot, ff, step, rising):
+        start, count = pieces(octs, rising)[step]
         return pltpu.make_async_remote_copy(
-            src_ref=f_hbm.at[rows_of(o), half_at(which)], dst_ref=dst.at[rows_of(o), :],
-            send_sem=fsend.at[slot, o], recv_sem=frecv.at[slot, o],
+            src_ref=f_hbm.at[start:start + count, half_at(which)], dst_ref=dst.at[start:start + count, :],
+            send_sem=fsend.at[slot, step], recv_sem=frecv.at[slot, step],
             device_id=dev(ff, p), device_id_type=MESH,
         )
 
-    def to_mate(o):
-        return field_copy(1 - odd, xbuf, 0, mate, o)
-
-    def to_lower(o):
-        return field_copy(0, ubuf, 1, f - 2, o)
-
-    def to_upper(o):
-        return field_copy(1, dbuf, 2, f + 2, o)
-
-    for o in range(octs):
-        to_mate(octs - 1 - o).start()
+    def to_mate(step):
+        return field_copy(1 - odd, xbuf, 0, mate, step, False)
+
+    def to_lower(step):
+        return field_copy(0, ybuf, 1, f - 2, step, True)
+
+    def to_upper(step):
+        return field_copy(1, ybuf, 1, f + 2, step, False)
+
+    steps = octs + 1
+    for step in range(steps):
+        to_mate(step).start()
 
         @pl.when(has_d)
-        def _(o=o):
-            to_lower(o).start()
+        def _(step=step):
+            to_lower(step).start()
 
         @pl.when(has_u)
-        def _(o=o):
-            to_upper(octs - 1 - o).start()
+        def _(step=step):
+            to_upper(step).start()
 
     for far in range(1, nz - 1):
         @pl.when(jnp.logical_and(above, z >= far))
@@ -188,24 +260,24 @@
             w = jnp.where(index == value, jnp.float32(entry), w)
         return w
 
-    def scale(src, dst, where, o, n):
+    def scale(src, dst, where, start, count):
         w = weight_at(where)
 
         def step(i, carry):
-            at = pl.ds(pl.multiple_of(o * oct_rows + i * 32, 32), 32)
+            at = pl.ds(pl.multiple_of(start + i * 32, 32), 32)
             dst[at, :] = (src[at, :].astype(f32) * w).astype(bf16)
             return carry
 
-        lax.fori_loop(0, n * oct_rows // 32, step, 0)
+        lax.fori_loop(0, count // 32, step, 0)
 
     def gram(left, left_at, lo, n, right, right_at, ro, m, slot, rel):
-        tall = 2 if n % 2 == 0 else 1
-        first_col = rel * block + ro * oct_rows
+        tall = 256 if n % 256 == 0 else n
+        first_col = rel * block + ro
 
         def step(i, carry):
-            at = rows_of(lo + i * tall, tall)
-            acc[slot, at, first_col:first_col + m * oct_rows] = lax.dot_general(
-                left[at, left_at], right[ro * oct_rows:(ro + m) * oct_rows, right_at],
+            at = pl.ds(pl.multiple_of(lo + i * tall, 4 * COMP), tall)
+            acc[slot, at, first_col:first_col + m] = lax.dot_general(
+                left[at, left_at], right[ro:ro + m, right_at],
                 (((1,), (1,)), ((), ())), preferred_element_type=f32,
             )
             return carry
@@ -215,25 +287,19 @@
         else:
             lax.fori_loop(0, n // tall, step, 0)
 
-    def clear(slot, tile):
-        acc[slot, :, tile * LANES:(tile + 1) * LANES] = jnp.zeros((rows, LANES), f32)
-
-    clear(XG, octs - 1)
-    clear(XG, 2 * octs)
-    clear(DG, octs - 1)
-
-    @pl.when(odd == 0)
-    def _():
-        clear(DG, 2 * octs - 1)
-
-    @pl.when(odd == 1)
-    def _():
-        clear(OWN, octs)
-        clear(OWN, 2 * octs - 1)
-
-    @pl.when(jnp.logical_not(has_u))
-    def _():
-        clear(OWN, 2 * octs)
+    plans = [plan(role, octs, npan) for role in range(nf)]
+
+    def each_role(act):
+        for role in range(nf):
+            @pl.when(f == role)
+            def _(role=role):
+                act(role)
+
+    def clear(role):
+        for slot, tile in plans[role][1]:
+            acc[slot, :, tile * LANES:(tile + 1) * LANES] = jnp.zeros((rows, LANES), f32)
+
+    each_role(clear)
 
     def valid(slot, o, pp):
         t = o + pp
@@ -251,72 +317,108 @@
         upper = jnp.logical_or(t >= 2 * octs - 1, jnp.logical_and(odd == 1, low))
         return jnp.logical_and(has_d, upper)
 
-    def core_copy(slot, o, pp):
+    def span(o, h, n):
+        return pl.ds((2 * o + h) * (oct_rows // 2), n * (oct_rows // 2))
+
+    def core_copy(tile):
+        slot, o, h, n, pp = tile
         zd = pp // CORES
         return pltpu.make_async_remote_copy(
-            src_ref=away.at[slot, pp, rows_of(o), :], dst_ref=cxin.at[slot, zd, rows_of(o), :],
-            send_sem=csend.at[slot, zd, o], recv_sem=crecv.at[slot, zd, o],
+            src_ref=away.at[slot, zd, span(o, h, n), :], dst_ref=cxin.at[slot, zd, span(o, h, n), :],
+            send_sem=csend.at[slot, zd, 2 * o + h], recv_sem=crecv.at[slot, zd, 2 * o + h],
             device_id=dev(f, partner), device_id_type=MESH,
         )
 
-    def z_copy(slot, o, zd, source):
+    def z_copy(tile):
+        slot, o, h, n, pp = tile
+        zd = pp // CORES
         return pltpu.make_async_remote_copy(
-            src_ref=zout.at[slot, zd, rows_of(o), :], dst_ref=zin.at[slot, source, rows_of(o), :],
-            send_sem=zsend.at[slot, zd, o], recv_sem=zrecv.at[slot, source, o],
+            src_ref=zout.at[slot, zd, span(o, h, n), :], dst_ref=zin.at[slot, z, span(o, h, n), :],
+            send_sem=zsend.at[slot, zd, 2 * o + h], recv_sem=zrecv.at[slot, z, o],
             device_id=dev(f, zd * CORES + core), device_id_type=MESH,
         )
 
-    def walk(act, slot, o, t, n, do, dt):
-        def step(i, carry):
-            oo, tt = o + i * do, t + i * dt
-            act(slot, oo, tt - oo, tt)
-            return carry
-
-        if n > 0:
-            lax.fori_loop(0, n, step, 0)
-
-    def make(slot, o, pp, t):
-        lane = pl.multiple_of(t * LANES, LANES)
-        for c in range(8):
-            at = pl.ds(pl.multiple_of(o * oct_rows + c * COMP, COMP), COMP)
+    def from_z(slot, o, source):
+        return pltpu.make_async_remote_copy(
+            src_ref=zout.at[slot, z, rows_of(o), :], dst_ref=zin.at[slot, source, rows_of(o), :],
+            send_sem=zsend.at[slot, z, 2 * o], recv_sem=zrecv.at[slot, source, o],
+            device_id=dev(f, source * CORES + core), device_id_type=MESH,
+        )
+
+    def band(tile, put):
+        slot, o, h, n, pp = tile
+        lane = (o + pp) * LANES
+        for c in range(4 * h, 4 * (h + n)):
+            at = pl.ds(o * oct_rows + c * COMP, COMP)
             if c == 7:
-                value = acc[slot, at, pl.ds(pl.multiple_of(lane + LANES, LANES), LANES)]
+                value = acc[slot, at, lane + LANES:lane + 2 * LANES]
             else:
-                pair = acc[slot, at, pl.ds(lane, 2 * LANES)]
+                pair = acc[slot, at, lane:lane + 2 * LANES]
                 value = pltpu.roll(pair, 2 * LANES - COMP * (c + 1), 1)[:, :LANES]
-            keep[slot, pp, at, :] = value
-            away[slot, pp, at, :] = value.astype(bf16)
-
-        @pl.when(lax.rem(pp, CORES) != core)
-        def _():
-            core_copy(slot, o, pp).start()
-
-    def join(slot, o, pp, t):
-        @pl.when(lax.rem(pp, CORES) == core)
-        def _():
-            zd = pp // CORES
-            core_copy(slot, o, pp).wait_recv()
-            both = keep[slot, pp, rows_of(o), :] + cxin[slot, zd, rows_of(o), :].astype(f32)
-
-            @pl.when(z == zd)
-            def _():
-                total[slot, rows_of(o), :] = both
-
-            @pl.when(z != zd)
-            def _():
-                zout[slot, zd, rows_of(o), :] = both.astype(bf16)
-                z_copy(slot, o, zd, z).start()
-
-    def both_ways(jobs):
-        for act in (make, join):
-            for job in jobs:
-                if len(job) == 2:
-                    @pl.when(job[0])
-                    def _(job=job, act=act):
-                        for inner in job[1]:
-                            walk(act, *inner)
-                else:
-                    walk(act, *job)
+            put(at, value)
+
+    def send(tile):
+        slot, zd = tile[0], tile[4] // CORES
+
+        def put(at, value):
+            away[slot, zd, at, :] = value.astype(bf16)
+
+        band(tile, put)
+        core_copy(tile).start()
+
+    def hold(tile):
+        slot, zd = tile[0], tile[4] // CORES
+
+        def put(at, value):
+            keep[slot, zd, at, :] = value
+
+        band(tile, put)
+
+    def join(tile):
+        slot, o, h, n, pp = tile
+        zd = pp // CORES
+        at = span(o, h, n)
+        core_copy(tile).wait_recv()
+        both = keep[slot, zd, at, :] + cxin[slot, zd, at, :].astype(f32)
+
+        @pl.when(z == zd)
+        def _():
+            total[slot, at, :] = both
+
+        @pl.when(z != zd)
+        def _():
+            zout[slot, zd, at, :] = both.astype(bf16)
+            z_copy(tile).start()
+
+    def sent(tile):
+        core_copy(tile).wait_send()
+
+    def joined(tile):
+        @pl.when(z != tile[4] // CORES)
+        def _():
+            z_copy(tile).wait_send()
+
+    def tiles(jobs):
+        def run(role):
+            for side in range(CORES):
+                work = []
+                for act, mine, batch in jobs:
+                    for tile in plans[role][0].get(batch, []):
+                        if (tile[4] % CORES == side) == mine:
+                            work.append((act, tile))
+                if work:
+                    @pl.when(core == side)
+                    def _(work=work):
+                        for act, tile in work:
+                            act(tile)
+
+        each_role(run)
+
+    def finish(*batches):
+        tiles([(hold, True, b) for b in batches] + [(join, True, b) for b in batches])
+
+    def drain(*batches):
+        tiles([(sent, False, b) for b in batches] + [(joined, True, b) for b in batches])
 
     for load in loads:
         load.wait()
@@ -324,75 +426,56 @@
     first = pl.ds(0, half)
     second = pl.ds(half, half)
     even_now, odd_now = odd == 0, odd == 1
-    scale(own, scaled, everything, 0, octs)
-    gram(scaled, everything, 0, octs, own, everything, 0, octs, OWN, 0)
-    jobs = [(OWN, 0, t, t + 1, 1, 0) for t in range(octs - 1)]
-    jobs.append((odd_now, [(OWN, 0, octs - 1, octs, 1, 0)]))
-    both_ways(jobs)
-
-    for i in range(octs):
-        x = octs - 1 - i
-        last = i == octs - 1
-        to_mate(x).wait_recv()
-        scale(xbuf, xs, half_at(odd), x, 1)
-        jobs = []
+    scale(own, scaled, everything, 0, rows)
+    gram(scaled, everything, 0, rows, own, everything, 0, rows, OWN, 0)
+    tiles([(send, False, 0)])
+    finish(0)
+
+    for step in range(steps):
+        x_from, x_rows = pieces(octs, False)[step]
+        up_from, up_rows = pieces(octs, True)[step]
+        x_end, up_end = x_from + x_rows, up_from + up_rows
+        now, late = 2 * step + 2, 2 * step + 3
+        drain(*((0,) if step == 0 else (now - 2, late - 2)))
+        to_mate(step).wait_recv()
 
         @pl.when(odd_now)
-        def _(x=x):
-            gram(xs, first, x, 1, own, second, 0, octs, XG, 1)
-
-        jobs.append((odd_now, [(XG, x, octs - 1, octs + 1, 0, 1)]))
+        def _():
+            scale(xbuf, xs, second, x_from, x_rows)
+            gram(xs, first, x_from, x_rows, own, second, 0, rows, XG, 1)
 
         @pl.when(even_now)
-        def _(x=x):
-            gram(scaled, first, 0, octs, xbuf, first, x, 1, OWN, 1)
+        def _():
+            gram(scaled, first, 0, rows, xbuf, first, x_from, x_rows, OWN, 1)
+
+        tiles([(send, False, now)])
 
         @pl.when(has_u)
-        def _(i=i):
-            to_lower(i).wait_recv()
-            gram(scaled, first, i, octs - i, ubuf, first, i, 1, OWN, 2)
+        def _():
+            to_lower(step).wait_recv()
+            gram(scaled, first, up_from, rows - up_from, ybuf, first, up_from, up_rows, OWN, 2)
 
         @pl.when(jnp.logical_and(has_u, even_now))
-        def _(i=i, x=x):
-            gram(xs, first, x, 1, ubuf, first, 0, i + 1, XG, 1)
-            if i:
-                gram(xs, first, x + 1, i, ubuf, first, i, 1, XG, 1)
-
-        mixed = [(XG, x, octs - 1, i + 1 + last, 0, 1), (XG, x + 1, octs - 1 + i, i, 1, 0)]
-        if last:
-            mixed.append((XG, x + 1, 2 * octs - 1, i, 1, 0))
-        jobs.append((jnp.logical_and(has_u, even_now), mixed))
+        def _():
+            scale(xbuf, xs, first, x_from, x_rows)
+            gram(xs, first, x_from, x_rows, ybuf, first, 0, up_end, XG, 1)
+            if x_end < rows:
+                gram(xs, first, x_end, rows - x_end, ybuf, first, up_from, up_rows, XG, 1)
 
         @pl.when(has_d)
-        def _(x=x):
-            to_upper(x).wait_recv()
-            scale(dbuf, ds, second, x, 1)
-            gram(ds, first, x, 1, own, second, 0, x + 1, DG, 2)
+        def _():
+            to_upper(step).wait_recv()
+            scale(ybuf, ys, second, x_from, x_rows)
+            gram(ys, first, x_from, x_rows, own, second, 0, x_end, DG, 2)
 
         @pl.when(jnp.logical_and(has_d, odd_now))
-        def _(i=i, x=x):
-            gram(ds, first, x, 1, xbuf, first, x, i + 1, DG, 1)
-            if i:
-                gram(ds, first, x + 1, i, xbuf, first, x, 1, DG, 1)
-
-        mixed = [
-            (DG, x, octs + x - last, i + 1 + last, 0, 1),
-            (DG, x + 1, octs + x, i, 1, 0),
-            (DG, x, 2 * octs, x, 0, 1),
-        ]
-        if last:
-            mixed.append((DG, x + 1, octs - 1, i, 1, 0))
-        jobs.append((jnp.logical_and(has_d, odd_now), mixed))
-        jobs.append((jnp.logical_and(has_d, even_now), [(DG, x, 2 * octs - 1, x + 1, 0, 1)]))
-        own_even = [(OWN, 0, octs + x, octs, 1, 0)]
-        if last:
-            own_even.append((OWN, 0, octs - 1, octs, 1, 0))
-        jobs.append((even_now, own_even))
-        if i == 0:
-            jobs.append((jnp.logical_and(has_u, odd_now), [(OWN, 0, 2 * octs - 1, octs, 1, 0)]))
-        else:
-            jobs.append((has_u, [(OWN, i, 2 * octs - 1 + i, octs - i, 1, 0)]))
-        both_ways(jobs)
+        def _():
+            gram(ys, first, x_from, x_rows, xbuf, first, x_from, rows - x_from, DG, 1)
+            if x_end < rows:
+                gram(ys, first, x_end, rows - x_end, xbuf, first, x_from, x_rows, DG, 1)
+
+        tiles([(send, False, late)])
+        finish(now, late)
 
     def forward(slot, ff, o):
         return pltpu.make_async_remote_copy(
@@ -410,7 +493,7 @@
                 value = total[slot, rows_of(o), :]
                 for hop in range(1, nz):
                     source = lax.rem(z + hop, nz)
-                    z_copy(slot, o, z, source).wait_recv()
+                    from_z(slot, o, source).wait_recv()
                     value = value + zin[slot, source, rows_of(o), :].astype(f32)
                 total[slot, rows_of(o), :] = value
                 if target is not None:
@@ -429,28 +512,6 @@
     settle(XG, mate)
     settle(DG, f - 2)
     settle(OWN, None)
-
-    def drain(slot):
-        def step(i, carry):
-            pp, o = i // octs, lax.rem(i, octs)
-            zd = pp // CORES
-
-            @pl.when(valid(slot, o, pp))
-            def _():
-                @pl.when(lax.rem(pp, CORES) != core)
-                def _():
-                    core_copy(slot, o, pp).wait_send()
-
-                @pl.when(jnp.logical_and(lax.rem(pp, CORES) == core, z != zd))
-                def _():
-                    z_copy(slot, o, zd, z).wait_send()
-
-            return carry
-
-        lax.fori_loop(0, npan * octs, step, 0)
-
-    for slot in (OWN, XG, DG):
-        drain(slot)
 
     mate_gives = jnp.logical_or(odd == 0, f + 1 < nf)
 
@@ -505,17 +566,19 @@
             start = (k * (COMP // 8) + h) * LANES
             out_ref[:, start:start + LANES] = jnp.where(live, values[k] * norm, 0.0)
 
+    drain(2 * steps, 2 * steps + 1)
+    for step in range(steps):
+        to_mate(step).wait_send()
+
+        @pl.when(has_d)
+        def _(step=step):
+            to_lower(step).wait_send()
+
+        @pl.when(has_u)
+        def _(step=step):
+            to_upper(step).wait_send()
+
     def close(o, carry):
-        to_mate(o).wait_send()
-
-        @pl.when(has_d)
-        def _():
-            to_lower(o).wait_send()
-
-        @pl.when(has_u)
-        def _():
-            to_upper(o).wait_send()
-
         @pl.when(valid(XG, o, p))
         def _():
             forward(XG, mate, o).wait_send()
@@ -551,10 +614,9 @@
             pltpu.VMEM((rows, half), bf16),
             pltpu.VMEM((rows, half), bf16),
             pltpu.VMEM((rows, half), bf16),
-            pltpu.VMEM((rows, half), bf16),
             pltpu.VMEM((3, rows, (REACH + 1) * rows), f32),
-            pltpu.VMEM((3, npan, rows, LANES), f32),
-            pltpu.VMEM((3, npan, rows, LANES), bf16),
+            pltpu.VMEM((3, nz, rows, LANES), f32),
+            pltpu.VMEM((3, nz, rows, LANES), bf16),
             pltpu.VMEM((3, nz, rows, LANES), bf16),
             pltpu.VMEM((3, nz, rows, LANES), bf16),
             pltpu.VMEM((3, nz, rows, LANES), bf16),
@@ -566,9 +628,9 @@
             pltpu.VMEM((1, freqs), jnp.int32),
             pltpu.SemaphoreType.REGULAR((2, max(nz - 2, 1))),
             dma((3,)),
-            dma((3, octs)), dma((3, octs)),
-            dma((3, nz, octs)), dma((3, nz, octs)),
-            dma((3, nz, octs)), dma((3, nz, octs)),
+            dma((2, octs + 1)), dma((2, octs + 1)),
+            dma((3, nz, 2 * octs)), dma((3, nz, 2 * octs)),
+            dma((3, nz, 2 * octs)), dma((3, nz, octs)),
             dma((3, octs)), dma((3, octs)),
         ],
         compiler_params=pltpu.CompilerParams(
@@ -580,7 +642,7 @@
 def local(nf, npan, fields, quad_index, band_width):
     freqs, comp, panels = fields.shape
     share = REACH * freqs * comp // npan
-    fits = nf % 2 == 0 and npan % CORES == 0 and share == LANES and freqs % 8 == 0 and panels % (4 * LANES) == 0
+    fits = nf == 2 * REACH and npan % CORES == 0 and share == LANES and freqs % 8 == 0 and panels % (4 * LANES) == 0
     if not fits:
         return plain(fields, quad_index, band_width)
     return fused(nf, npan, fields, quad_index, band_width)

time: 48.8 us -> 55 us (1.13)
  the two profiles are of different devices: /device:TPU:0 before, /device:TPU:26 now
where the time goes in v2:
time: 55 us; the launch traced here: 54.9 us
  Pallas kernels  53.2 us (97%)
  local copies, waits for them, and re-layouts  1.67 us (3%)
    pallas_call x1, Pallas kernels, fused(): pl.pallas_call(functools.partial(kernel, nf, npan), out_shape=jax.ShapeDt...  53.2 us
    unnamed x1, local copies, waits for them, and re-layouts  1.67 us

profile of v2, /device:TPU:26, one launch (start us, length us, event | category | flops | bytes accessed | tf_op | source)
XLA Modules:
  0.0 54.9 jit_solution(12273782792563704571)
XLA Ops:
  0.0 53.2 %shard_map.37 = f32[32,2048]{1,0:T(8,128)} custom-call(bf16[512,2048]{1,0:T(8,128)(2,1)} %bitcast.3, s32[1,2048]{1,0:T(1,128)} %bitcast.4, s32[1,32]{1,0:T(1,128)} %bitcast.5), custom_call_target="tpu_custom_call" | custom-call | tf_op jit(solution)/shard_map/pallas_call | solution.py:605
  53.2 1.7 %copy.5 = f32[32,2048]{1,0:T(8,128)} copy(f32[32,2048]{1,0:T(8,128)} %shard_map.37) | data formatting | bytes 524288

commit v3 on v1

--- a/solution.py
+++ b/solution.py
@@ -65,9 +65,50 @@
 OWN, XG, DG = 0, 1, 2
 
 
+def plan(role, octs, npan):
+    even, low = role % 2 == 0, role < 2
+
+    def due(slot, row, col):
+        block, col = divmod(col, octs)
+        x_row, x_col = octs - row, octs - col
+        y_row, y_col = x_row, col + 1 if low else x_col
+        if slot == OWN:
+            if block == 0:
+                return 0
+            if block == 1 and even:
+                return x_col
+            if block == 2 and low:
+                return y_col
+        if slot == XG and block == 1:
+            if not even:
+                return x_row
+            if low:
+                return max(x_row, y_col)
+        if slot == DG and not low:
+            if block == 2:
+                return y_row
+            if block == 1 and not even:
+                return max(y_row, x_col)
+        return None
+
+    batches = [[[] for _ in range(octs + 1)] for _ in range(CORES)]
+    blank = set()
+    for slot in (OWN, XG, DG):
+        for o in range(octs):
+            for pp in range(npan):
+                t = o + pp
+                times = [due(slot, o, t), due(slot, o, t + 1)]
+                if times == [None, None]:
+                    continue
+                blank.update((slot, t + k) for k in range(2) if times[k] is None)
+                last = max(time for time in times if time is not None)
+                batches[pp % CORES][last].append((slot, o, pp // CORES))
+    return batches, sorted(blank)
+
+
 def kernel(
     nf, npan, f_hbm, q_hbm, bw_hbm, out_ref,
-    own, scaled, xbuf, ubuf, dbuf, xs, ds, acc, keep, away, cxin, zout, zin, total, give, fwd, fin,
+    own, scaled, xbuf, ybuf, xs, ys, acc, keep, away, cxin, zout, zin, total, give, fwd, fin,
     q_ref, bw_ref, near, local_sem, fsend, frecv, csend, crecv, zsend, zrecv, gsend, grecv,
 ):
     rows, panels = own.shape
@@ -137,32 +178,68 @@
     def rows_of(o, n=1):
         return pl.ds(pl.multiple_of(o * oct_rows, oct_rows), n * oct_rows)
 
-    def field_copy(which, dst, slot, ff, o):
+    def field_copy(which, dst, slot, ff, step, o):
         return pltpu.make_async_remote_copy(
             src_ref=f_hbm.at[rows_of(o), half_at(which)], dst_ref=dst.at[rows_of(o), :],
-            send_sem=fsend.at[slot, o], recv_sem=frecv.at[slot, o],
+            send_sem=fsend.at[slot, step], recv_sem=frecv.at[slot, step],
             device_id=dev(ff, p), device_id_type=MESH,
         )
 
-    def to_mate(o):
-        return field_copy(1 - odd, xbuf, 0, mate, o)
-
-    def to_lower(o):
-        return field_copy(0, ubuf, 1, f - 2, o)
-
-    def to_upper(o):
-        return field_copy(1, dbuf, 2, f + 2, o)
-
-    for o in range(octs):
-        to_mate(octs - 1 - o).start()
+    def to_mate(step):
+        return field_copy(1 - odd, xbuf, 0, mate, step, octs - 1 - step)
+
+    def to_lower(step):
+        return field_copy(0, ybuf, 1, f - 2, step, step)
+
+    def to_upper(step):
+        return field_copy(1, ybuf, 1, f + 2, step, octs - 1 - step)
+
+    def depart(step, carry):
+        to_mate(step).start()
 
         @pl.when(has_d)
-        def _(o=o):
-            to_lower(o).start()
+        def _():
+            to_lower(step).start()
 
         @pl.when(has_u)
-        def _(o=o):
-            to_upper(octs - 1 - o).start()
+        def _():
+            to_upper(step).start()
+
+        return carry
+
+    lax.fori_loop(0, octs, depart, 0)
+
+    plans = [plan(role, octs, npan) for role in range(nf)]
+    base = 1
+    while base < 3 * octs * nz:
+        base *= 2
+    per = 1
+    while base ** (per + 1) <= 2 ** 31:
+        per += 1
+    most = max(len(found) for lists, _ in plans for side in lists for found in side)
+    words = max(-(-most // per), 1)
+
+    def packed(found, w):
+        value = 0
+        for slot, o, zd in reversed(found[w * per:(w + 1) * per]):
+            value = value * base + (slot * octs + o) * nz + zd
+        return value
+
+    def mine(seat, of):
+        value = jnp.int32(0)
+        for role in range(nf):
+            for side in range(CORES):
+                value = jnp.where(seat == role * CORES + side, jnp.int32(of(plans[role][0][side])), value)
+        return value
+
+    orders = []
+    for seat in (f * CORES + 1 - core, f * CORES + core):
+        orders.append([
+            [mine(seat, lambda lists: len(lists[b]))]
+            + [mine(seat, lambda lists: packed(lists[b], w)) for w in range(words)]
+            for b in range(octs + 1)
+        ])
+    LEAVE, STAY = orders
 
     for far in range(1, nz - 1):
         @pl.when(jnp.logical_and(above, z >= far))
@@ -188,24 +265,25 @@
             w = jnp.where(index == value, jnp.float32(entry), w)
         return w
 
-    def scale(src, dst, where, o, n):
+    def scale(src, dst, where, start, count):
         w = weight_at(where)
 
         def step(i, carry):
-            at = pl.ds(pl.multiple_of(o * oct_rows + i * 32, 32), 32)
+            at = pl.ds(pl.multiple_of(start + i * 32, 32), 32)
             dst[at, :] = (src[at, :].astype(f32) * w).astype(bf16)
             return carry
 
-        lax.fori_loop(0, n * oct_rows // 32, step, 0)
+        lax.fori_loop(0, count // 32, step, 0)
 
     def gram(left, left_at, lo, n, right, right_at, ro, m, slot, rel):
-        tall = 2 if n % 2 == 0 else 1
-        first_col = rel * block + ro * oct_rows
+        tall = min(n, 256)
+        cols = pl.ds(pl.multiple_of(rel * block + ro, LANES), m)
+        over = pl.ds(ro, m)
 
         def step(i, carry):
-            at = rows_of(lo + i * tall, tall)
-            acc[slot, at, first_col:first_col + m * oct_rows] = lax.dot_general(
-                left[at, left_at], right[ro * oct_rows:(ro + m) * oct_rows, right_at],
+            at = pl.ds(pl.multiple_of(lo + i * tall, oct_rows), tall)
+            acc[slot, at, cols] = lax.dot_general(
+                left[at, left_at], right[over, right_at],
                 (((1,), (1,)), ((), ())), preferred_element_type=f32,
             )
             return carry
@@ -215,25 +293,11 @@
         else:
             lax.fori_loop(0, n // tall, step, 0)
 
-    def clear(slot, tile):
-        acc[slot, :, tile * LANES:(tile + 1) * LANES] = jnp.zeros((rows, LANES), f32)
-
-    clear(XG, octs - 1)
-    clear(XG, 2 * octs)
-    clear(DG, octs - 1)
-
-    @pl.when(odd == 0)
-    def _():
-        clear(DG, 2 * octs - 1)
-
-    @pl.when(odd == 1)
-    def _():
-        clear(OWN, octs)
-        clear(OWN, 2 * octs - 1)
-
-    @pl.when(jnp.logical_not(has_u))
-    def _():
-        clear(OWN, 2 * octs)
+    for role in range(nf):
+        @pl.when(f == role)
+        def _(role=role):
+            for slot, tile in plans[role][1]:
+                acc[slot, :, tile * LANES:(tile + 1) * LANES] = jnp.zeros((rows, LANES), f32)
 
     def valid(slot, o, pp):
         t = o + pp
@@ -251,10 +315,9 @@
         upper = jnp.logical_or(t >= 2 * octs - 1, jnp.logical_and(odd == 1, low))
         return jnp.logical_and(has_d, upper)
 
-    def core_copy(slot, o, pp):
-        zd = pp // CORES
+    def core_copy(slot, o, zd):
         return pltpu.make_async_remote_copy(
-            src_ref=away.at[slot, pp, rows_of(o), :], dst_ref=cxin.at[slot, zd, rows_of(o), :],
+            src_ref=away.at[slot, zd, rows_of(o), :], dst_ref=cxin.at[slot, zd, rows_of(o), :],
             send_sem=csend.at[slot, zd, o], recv_sem=crecv.at[slot, zd, o],
             device_id=dev(f, partner), device_id_type=MESH,
         )
@@ -266,17 +329,8 @@
             device_id=dev(f, zd * CORES + core), device_id_type=MESH,
         )
 
-    def walk(act, slot, o, t, n, do, dt):
-        def step(i, carry):
-            oo, tt = o + i * do, t + i * dt
-            act(slot, oo, tt - oo, tt)
-            return carry
-
-        if n > 0:
-            lax.fori_loop(0, n, step, 0)
-
-    def make(slot, o, pp, t):
-        lane = pl.multiple_of(t * LANES, LANES)
+    def band(slot, o, zd, side, put):
+        lane = pl.multiple_of((o + zd * CORES + side) * LANES, LANES)
         for c in range(8):
             at = pl.ds(pl.multiple_of(o * oct_rows + c * COMP, COMP), COMP)
             if c == 7:
@@ -284,115 +338,132 @@
             else:
                 pair = acc[slot, at, pl.ds(lane, 2 * LANES)]
                 value = pltpu.roll(pair, 2 * LANES - COMP * (c + 1), 1)[:, :LANES]
-            keep[slot, pp, at, :] = value
-            away[slot, pp, at, :] = value.astype(bf16)
-
-        @pl.when(lax.rem(pp, CORES) != core)
-        def _():
-            core_copy(slot, o, pp).start()
-
-    def join(slot, o, pp, t):
-        @pl.when(lax.rem(pp, CORES) == core)
-        def _():
-            zd = pp // CORES
-            core_copy(slot, o, pp).wait_recv()
-            both = keep[slot, pp, rows_of(o), :] + cxin[slot, zd, rows_of(o), :].astype(f32)
-
-            @pl.when(z == zd)
-            def _():
-                total[slot, rows_of(o), :] = both
-
-            @pl.when(z != zd)
-            def _():
-                zout[slot, zd, rows_of(o), :] = both.astype(bf16)
-                z_copy(slot, o, zd, z).start()
-
-    def both_ways(jobs):
-        for act in (make, join):
-            for job in jobs:
-                if len(job) == 2:
-                    @pl.when(job[0])
-                    def _(job=job, act=act):
-                        for inner in job[1]:
-                            walk(act, *inner)
-                else:
-                    walk(act, *job)
-
-    for load in loads:
-        load.wait()
+            put(at, value)
+
+    def send(slot, o, zd):
+        def put(at, value):
+            away[slot, zd, at, :] = value.astype(bf16)
+
+        band(slot, o, zd, 1 - core, put)
+        core_copy(slot, o, zd).start()
+
+    def hold(slot, o, zd):
+        def put(at, value):
+            keep[slot, zd, at, :] = value
+
+        band(slot, o, zd, core, put)
+
+    def join(slot, o, zd):
+        at = rows_of(o)
+        core_copy(slot, o, zd).wait_recv()
+        both = keep[slot, zd, at, :] + cxin[slot, zd, at, :].astype(f32)
+
+        @pl.when(z == zd)
+        def _():
+            total[slot, at, :] = both
+
+        @pl.when(z != zd)
+        def _():
+            zout[slot, zd, at, :] = both.astype(bf16)
+            z_copy(slot, o, zd, z).start()
+
+    def sent(slot, o, zd):
+        core_copy(slot, o, zd).wait_send()
+
+    def joined(slot, o, zd):
+        @pl.when(z != zd)
+        def _():
+            z_copy(slot, o, zd, z).wait_send()
+
+    def each(act, order, b):
+        chosen = order[0]
+        for bb in range(1, octs + 1):
+            chosen = [jnp.where(b == bb, new, old) for new, old in zip(order[bb], chosen)]
+
+        def step(k, carry):
+            code = lax.rem(carry[0], base)
+            carry = (lax.div(carry[0], base),) + carry[1:]
+            fresh = lax.rem(k + 1, per) == 0
+            carry = tuple(jnp.where(fresh, new, old) for new, old in zip(carry[1:] + carry[-1:], carry))
+            act(lax.div(code, octs * nz), lax.rem(lax.div(code, nz), octs), lax.rem(code, nz))
+            return carry
+
+        lax.fori_loop(0, chosen[0], step, tuple(chosen[1:]))
+
     everything = pl.ds(0, panels)
     first = pl.ds(0, half)
     second = pl.ds(half, half)
     even_now, odd_now = odd == 0, odd == 1
-    scale(own, scaled, everything, 0, octs)
-    gram(scaled, everything, 0, octs, own, everything, 0, octs, OWN, 0)
-    jobs = [(OWN, 0, t, t + 1, 1, 0) for t in range(octs - 1)]
-    jobs.append((odd_now, [(OWN, 0, octs - 1, octs, 1, 0)]))
-    both_ways(jobs)
-
-    for i in range(octs):
-        x = octs - 1 - i
-        last = i == octs - 1
-        to_mate(x).wait_recv()
-        scale(xbuf, xs, half_at(odd), x, 1)
-        jobs = []
-
-        @pl.when(odd_now)
-        def _(x=x):
-            gram(xs, first, x, 1, own, second, 0, octs, XG, 1)
-
-        jobs.append((odd_now, [(XG, x, octs - 1, octs + 1, 0, 1)]))
-
-        @pl.when(even_now)
-        def _(x=x):
-            gram(scaled, first, 0, octs, xbuf, first, x, 1, OWN, 1)
-
-        @pl.when(has_u)
-        def _(i=i):
-            to_lower(i).wait_recv()
-            gram(scaled, first, i, octs - i, ubuf, first, i, 1, OWN, 2)
-
-        @pl.when(jnp.logical_and(has_u, even_now))
-        def _(i=i, x=x):
-            gram(xs, first, x, 1, ubuf, first, 0, i + 1, XG, 1)
-            if i:
-                gram(xs, first, x + 1, i, ubuf, first, i, 1, XG, 1)
-
-        mixed = [(XG, x, octs - 1, i + 1 + last, 0, 1), (XG, x + 1, octs - 1 + i, i, 1, 0)]
-        if last:
-            mixed.append((XG, x + 1, 2 * octs - 1, i, 1, 0))
-        jobs.append((jnp.logical_and(has_u, even_now), mixed))
-
-        @pl.when(has_d)
-        def _(x=x):
-            to_upper(x).wait_recv()
-            scale(dbuf, ds, second, x, 1)
-            gram(ds, first, x, 1, own, second, 0, x + 1, DG, 2)
-
-        @pl.when(jnp.logical_and(has_d, odd_now))
-        def _(i=i, x=x):
-            gram(ds, first, x, 1, xbuf, first, x, i + 1, DG, 1)
-            if i:
-                gram(ds, first, x + 1, i, xbuf, first, x, 1, DG, 1)
-
-        mixed = [
-            (DG, x, octs + x - last, i + 1 + last, 0, 1),
-            (DG, x + 1, octs + x, i, 1, 0),
-            (DG, x, 2 * octs, x, 0, 1),
-        ]
-        if last:
-            mixed.append((DG, x + 1, octs - 1, i, 1, 0))
-        jobs.append((jnp.logical_and(has_d, odd_now), mixed))
-        jobs.append((jnp.logical_and(has_d, even_now), [(DG, x, 2 * octs - 1, x + 1, 0, 1)]))
-        own_even = [(OWN, 0, octs + x, octs, 1, 0)]
-        if last:
-            own_even.append((OWN, 0, octs - 1, octs, 1, 0))
-        jobs.append((even_now, own_even))
-        if i == 0:
-            jobs.append((jnp.logical_and(has_u, odd_now), [(OWN, 0, 2 * octs - 1, octs, 1, 0)]))
-        else:
-            jobs.append((has_u, [(OWN, i, 2 * octs - 1 + i, octs - i, 1, 0)]))
-        both_ways(jobs)
+
+    def batch(b, carry):
+        @pl.when(b == 0)
+        def _():
+            for load in loads:
+                load.wait()
+            scale(own, scaled, everything, 0, rows)
+            gram(scaled, everything, 0, rows, own, everything, 0, rows, OWN, 0)
+
+        @pl.when(b > 0)
+        def _():
+            step = b - 1
+            down = pl.multiple_of((octs - 1 - step) * oct_rows, oct_rows)
+            up = pl.multiple_of(step * oct_rows, oct_rows)
+            to_mate(step).wait_recv()
+
+            @pl.when(odd_now)
+            def _():
+                scale(xbuf, xs, second, down, oct_rows)
+                gram(xs, first, down, oct_rows, own, second, 0, rows, XG, 1)
+
+            @pl.when(even_now)
+            def _():
+                gram(scaled, first, 0, rows, xbuf, first, down, oct_rows, OWN, 1)
+
+            @pl.when(has_u)
+            def _():
+                to_lower(step).wait_recv()
+                gram(scaled, first, 0, rows, ybuf, first, up, oct_rows, OWN, 2)
+
+            @pl.when(jnp.logical_and(has_u, even_now))
+            def _():
+                scale(xbuf, xs, first, down, oct_rows)
+
+                def cross(j, carry):
+                    gram(xs, first, down, oct_rows, ybuf, first, pl.multiple_of(j * oct_rows, oct_rows), oct_rows, XG, 1)
+                    gram(xs, first, pl.multiple_of((octs - 1 - j) * oct_rows, oct_rows), oct_rows, ybuf, first, up, oct_rows, XG, 1)
+                    return carry
+
+                lax.fori_loop(0, b, cross, 0)
+
+            @pl.when(has_d)
+            def _():
+                to_upper(step).wait_recv()
+                scale(ybuf, ys, second, down, oct_rows)
+                gram(ys, first, down, oct_rows, own, second, 0, rows, DG, 2)
+
+            @pl.when(jnp.logical_and(has_d, odd_now))
+            def _():
+                def cross(j, carry):
+                    there = pl.multiple_of((octs - 1 - j) * oct_rows, oct_rows)
+                    gram(ys, first, down, oct_rows, xbuf, first, there, oct_rows, DG, 1)
+                    gram(ys, first, there, oct_rows, xbuf, first, down, oct_rows, DG, 1)
+                    return carry
+
+                lax.fori_loop(0, b, cross, 0)
+
+        each(send, LEAVE, b)
+        each(hold, STAY, b)
+        each(join, STAY, b)
+        return carry
+
+    lax.fori_loop(0, octs + 1, batch, 0)
+
+    def drain(b, carry):
+        each(sent, LEAVE, b)
+        each(joined, STAY, b)
+        return carry
+
+    lax.fori_loop(0, octs, drain, 0)
 
     def forward(slot, ff, o):
         return pltpu.make_async_remote_copy(
@@ -429,28 +500,6 @@
     settle(XG, mate)
     settle(DG, f - 2)
     settle(OWN, None)
-
-    def drain(slot):
-        def step(i, carry):
-            pp, o = i // octs, lax.rem(i, octs)
-            zd = pp // CORES
-
-            @pl.when(valid(slot, o, pp))
-            def _():
-                @pl.when(lax.rem(pp, CORES) != core)
-                def _():
-                    core_copy(slot, o, pp).wait_send()
-
-                @pl.when(jnp.logical_and(lax.rem(pp, CORES) == core, z != zd))
-                def _():
-                    z_copy(slot, o, zd, z).wait_send()
-
-            return carry
-
-        lax.fori_loop(0, npan * octs, step, 0)
-
-    for slot in (OWN, XG, DG):
-        drain(slot)
 
     mate_gives = jnp.logical_or(odd == 0, f + 1 < nf)
 
@@ -505,6 +554,8 @@
             start = (k * (COMP // 8) + h) * LANES
             out_ref[:, start:start + LANES] = jnp.where(live, values[k] * norm, 0.0)
 
+    drain(octs, 0)
+
     def close(o, carry):
         to_mate(o).wait_send()
 
@@ -551,10 +602,9 @@
             pltpu.VMEM((rows, half), bf16),
             pltpu.VMEM((rows, half), bf16),
             pltpu.VMEM((rows, half), bf16),
-            pltpu.VMEM((rows, half), bf16),
             pltpu.VMEM((3, rows, (REACH + 1) * rows), f32),
-            pltpu.VMEM((3, npan, rows, LANES), f32),
-            pltpu.VMEM((3, npan, rows, LANES), bf16),
+            pltpu.VMEM((3, nz, rows, LANES), f32),
+            pltpu.VMEM((3, nz, rows, LANES), bf16),
             pltpu.VMEM((3, nz, rows, LANES), bf16),
             pltpu.VMEM((3, nz, rows, LANES), bf16),
             pltpu.VMEM((3, nz, rows, LANES), bf16),
@@ -566,7 +616,7 @@
             pltpu.VMEM((1, freqs), jnp.int32),
             pltpu.SemaphoreType.REGULAR((2, max(nz - 2, 1))),
             dma((3,)),
-            dma((3, octs)), dma((3, octs)),
+            dma((2, octs)), dma((2, octs)),
             dma((3, nz, octs)), dma((3, nz, octs)),
             dma((3, nz, octs)), dma((3, nz, octs)),
             dma((3, octs)), dma((3, octs)),
@@ -580,7 +630,7 @@
 def local(nf, npan, fields, quad_index, band_width):
     freqs, comp, panels = fields.shape
     share = REACH * freqs * comp // npan
-    fits = nf % 2 == 0 and npan % CORES == 0 and share == LANES and freqs % 8 == 0 and panels % (4 * LANES) == 0
+    fits = nf == 2 * REACH and npan % CORES == 0 and share == LANES and freqs % 8 == 0 and panels % (4 * LANES) == 0
     if not fits:
         return plain(fields, quad_index, band_width)
     return fused(nf, npan, fields, quad_index, band_width)

time: 48.8 us -> 47.4 us (0.971)
  Pallas kernels: 46.9 us -> 45.5 us
    pallas_call x1, Pallas kernels: 46.9 us -> 45.5 us  [fused(): pl.pallas_call(functools.partial(kernel, nf, npan), out_shape=jax.ShapeDt...]
where the time goes in v3:
time: 47.4 us; the launch traced here: 47.2 us
  Pallas kernels  45.5 us (96%)
  local copies, waits for them, and re-layouts  1.67 us (4%)
    pallas_call x1, Pallas kernels, fused(): pl.pallas_call(functools.partial(kernel, nf, npan), out_shape=jax.ShapeDt...  45.5 us
    unnamed x1, local copies, waits for them, and re-layouts  1.67 us

profile of v3, /device:TPU:0, one launch (start us, length us, event | category | flops | bytes accessed | tf_op | source)
XLA Modules:
  0.0 47.2 jit_solution(9363673448263461651)
XLA Ops:
  0.0 45.5 %shard_map.37 = f32[32,2048]{1,0:T(8,128)} custom-call(bf16[512,2048]{1,0:T(8,128)(2,1)} %bitcast.3, s32[1,2048]{1,0:T(1,128)} %bitcast.4, s32[1,32]{1,0:T(1,128)} %bitcast.5), custom_call_target="tpu_custom_call" | custom-call | tf_op jit(solution)/shard_map/pallas_call | solution.py:593
  45.5 1.7 %copy.5 = f32[32,2048]{1,0:T(8,128)} copy(f32[32,2048]{1,0:T(8,128)} %shard_map.37) | data formatting | bytes 524288

commit v4 on v3

--- a/solution.py
+++ b/solution.py
@@ -93,7 +93,7 @@
 
     batches = [[[] for _ in range(octs + 1)] for _ in range(CORES)]
     blank = set()
-    for slot in (OWN, XG, DG):
+    for slot in (XG, DG, OWN):
         for o in range(octs):
             for pp in range(npan):
                 t = o + pp
@@ -108,8 +108,8 @@
 
 def kernel(
     nf, npan, f_hbm, q_hbm, bw_hbm, out_ref,
-    own, scaled, xbuf, ybuf, xs, ys, acc, keep, away, cxin, zout, zin, total, give, fwd, fin,
-    q_ref, bw_ref, near, local_sem, fsend, frecv, csend, crecv, zsend, zrecv, gsend, grecv,
+    own, scaled, xbuf, ybuf, xs, ys, acc, keep, away, cxin, zout, zin, total, give, fwd, fin, relay, direct,
+    q_ref, bw_ref, near, local_sem, fsend, frecv, csend, crecv, zsend, zrecv, gsend, grecv, rsend, rrecv, drecv,
 ):
     rows, panels = own.shape
     half = panels // 2
@@ -229,34 +229,62 @@
         value = jnp.int32(0)
         for role in range(nf):
             for side in range(CORES):
-                value = jnp.where(seat == role * CORES + side, jnp.int32(of(plans[role][0][side])), value)
+                value = jnp.where(seat == role * CORES + side, jnp.int32(of(role, side)), value)
         return value
 
     orders = []
     for seat in (f * CORES + 1 - core, f * CORES + core):
         orders.append([
-            [mine(seat, lambda lists: len(lists[b]))]
-            + [mine(seat, lambda lists: packed(lists[b], w)) for w in range(words)]
+            [mine(seat, lambda role, side: len(plans[role][0][side][b]))]
+            + [mine(seat, lambda role, side: packed(plans[role][0][side][b], w)) for w in range(words)]
             for b in range(octs + 1)
         ])
     LEAVE, STAY = orders
-
-    for far in range(1, nz - 1):
+    busy = jnp.logical_or(jnp.logical_and(has_u, odd == 0), jnp.logical_and(has_d, odd == 1))
+
+    def crossing(role, side):
+        busy = (role < 2) == (role % 2 == 0)
+        return [tile for tile in plans[role][0][side][octs] if busy and tile[0] == XG]
+
+    passing = [mine(mate * CORES + core, lambda role, side: len(crossing(role, side)))]
+    passing += [mine(mate * CORES + core, lambda role, side: packed(crossing(role, side), w)) for w in range(words)]
+
+    def tell(far):
         @pl.when(jnp.logical_and(above, z >= far))
-        def _(far=far):
+        def _():
             pl.semaphore_signal(near.at[0, far - 1], inc=1, device_id=dev(f, p + CORES), device_id_type=MESH)
 
         @pl.when(jnp.logical_and(below, z + far < nz))
-        def _(far=far):
+        def _():
             pl.semaphore_signal(near.at[1, far - 1], inc=1, device_id=dev(f, p - CORES), device_id_type=MESH)
 
+    def hear(far):
         @pl.when(z > far)
-        def _(far=far):
+        def _():
             pl.semaphore_wait(near.at[0, far - 1], 1)
 
         @pl.when(z + 1 + far < nz)
-        def _(far=far):
+        def _():
             pl.semaphore_wait(near.at[1, far - 1], 1)
+
+    def late_bits(giver):
+        value = jnp.int32(0)
+        for role in range(nf):
+            for pp in range(npan):
+                bits = sum(2 ** o for _, o, zd in crossing(role, pp % CORES) if zd == pp // CORES)
+                if bits:
+                    value = jnp.where(jnp.logical_and(giver == role, p == pp), jnp.int32(bits), value)
+        return value
+
+    def is_late(bits, o):
+        picked = jnp.int32(0)
+        for oo in range(octs):
+            picked = jnp.where(o == oo, lax.rem(lax.div(bits, 2 ** oo), 2), picked)
+        return picked == 1
+
+    given = late_bits(f)
+    got = late_bits(mate)
+    tell(1)
 
     def weight_at(where):
         index = q_ref[:, where]
@@ -276,7 +304,7 @@
         lax.fori_loop(0, count // 32, step, 0)
 
     def gram(left, left_at, lo, n, right, right_at, ro, m, slot, rel):
-        tall = min(n, 256)
+        tall = n if panels > left_at.size else min(n, 256)
         cols = pl.ds(pl.multiple_of(rel * block + ro, LANES), m)
         over = pl.ds(ro, m)
 
@@ -340,69 +368,109 @@
                 value = pltpu.roll(pair, 2 * LANES - COMP * (c + 1), 1)[:, :LANES]
             put(at, value)
 
-    def send(slot, o, zd):
+    def send(slot, o, zd, b):
         def put(at, value):
             away[slot, zd, at, :] = value.astype(bf16)
 
         band(slot, o, zd, 1 - core, put)
         core_copy(slot, o, zd).start()
 
-    def hold(slot, o, zd):
+    def hold(slot, o, zd, b):
         def put(at, value):
             keep[slot, zd, at, :] = value
 
         band(slot, o, zd, core, put)
 
-    def join(slot, o, zd):
+    def straight(o, zd):
+        return pltpu.make_async_remote_copy(
+            src_ref=zout.at[XG, zd, rows_of(o), :], dst_ref=relay.at[zd, rows_of(o), :],
+            send_sem=zsend.at[XG, zd, o], recv_sem=rrecv.at[zd, o],
+            device_id=dev(mate, p), device_id_type=MESH,
+        )
+
+    def onward(o, zd, source):
+        return pltpu.make_async_remote_copy(
+            src_ref=relay.at[zd, rows_of(o), :], dst_ref=direct.at[source, rows_of(o), :],
+            send_sem=rsend.at[zd, o], recv_sem=drecv.at[source, o],
+            device_id=dev(f, zd * CORES + core), device_id_type=MESH,
+        )
+
+    def hand_on(slot, o, zd, b):
+        straight(o, zd).wait_recv()
+
+        @pl.when(z != zd)
+        def _():
+            onward(o, zd, z).start()
+
+    def handed(slot, o, zd, b):
+        @pl.when(z != zd)
+        def _():
+            onward(o, zd, z).wait_send()
+
+    def join(slot, o, zd, b):
         at = rows_of(o)
         core_copy(slot, o, zd).wait_recv()
         both = keep[slot, zd, at, :] + cxin[slot, zd, at, :].astype(f32)
 
-        @pl.when(z == zd)
+        away_now = jnp.logical_and(b == octs, jnp.logical_and(slot == XG, busy))
+
+        @pl.when(jnp.logical_and(z == zd, jnp.logical_not(away_now)))
         def _():
             total[slot, at, :] = both
 
-        @pl.when(z != zd)
+        @pl.when(jnp.logical_or(z != zd, away_now))
         def _():
             zout[slot, zd, at, :] = both.astype(bf16)
+
+        @pl.when(jnp.logical_and(z != zd, jnp.logical_not(away_now)))
+        def _():
             z_copy(slot, o, zd, z).start()
 
-    def sent(slot, o, zd):
+        @pl.when(away_now)
+        def _():
+            straight(o, zd).start()
+
+    def sent(slot, o, zd, b):
         core_copy(slot, o, zd).wait_send()
 
-    def joined(slot, o, zd):
-        @pl.when(z != zd)
+    def joined(slot, o, zd, b):
+        @pl.when(jnp.logical_or(z != zd, jnp.logical_and(b == octs, jnp.logical_and(slot == XG, busy))))
         def _():
             z_copy(slot, o, zd, z).wait_send()
 
-    def each(act, order, b):
-        chosen = order[0]
-        for bb in range(1, octs + 1):
-            chosen = [jnp.where(b == bb, new, old) for new, old in zip(order[bb], chosen)]
-
+    def walk(act, chosen, b):
         def step(k, carry):
             code = lax.rem(carry[0], base)
             carry = (lax.div(carry[0], base),) + carry[1:]
             fresh = lax.rem(k + 1, per) == 0
             carry = tuple(jnp.where(fresh, new, old) for new, old in zip(carry[1:] + carry[-1:], carry))
-            act(lax.div(code, octs * nz), lax.rem(lax.div(code, nz), octs), lax.rem(code, nz))
+            act(lax.div(code, octs * nz), lax.rem(lax.div(code, nz), octs), lax.rem(code, nz), b)
             return carry
 
         lax.fori_loop(0, chosen[0], step, tuple(chosen[1:]))
+
+    def each(act, order, b):
+        chosen = order[0]
+        for bb in range(1, octs + 1):
+            chosen = [jnp.where(b == bb, new, old) for new, old in zip(order[bb], chosen)]
+
+        walk(act, chosen, b)
 
     everything = pl.ds(0, panels)
     first = pl.ds(0, half)
     second = pl.ds(half, half)
     even_now, odd_now = odd == 0, odd == 1
 
+    for load in loads:
+        load.wait()
+    scale(own, scaled, everything, 0, rows)
+    for far in range(1, nz - 1):
+        hear(far)
+        if far + 1 < nz - 1:
+            tell(far + 1)
+    gram(scaled, everything, 0, rows, own, everything, 0, rows, OWN, 0)
+
     def batch(b, carry):
-        @pl.when(b == 0)
-        def _():
-            for load in loads:
-                load.wait()
-            scale(own, scaled, everything, 0, rows)
-            gram(scaled, everything, 0, rows, own, everything, 0, rows, OWN, 0)
-
         @pl.when(b > 0)
         def _():
             step = b - 1
@@ -422,34 +490,54 @@
             @pl.when(has_u)
             def _():
                 to_lower(step).wait_recv()
-                gram(scaled, first, 0, rows, ybuf, first, up, oct_rows, OWN, 2)
+
+                def below_up(i, carry):
+                    gram(scaled, first, pl.multiple_of(i * oct_rows, oct_rows), oct_rows, ybuf, first, up, oct_rows, OWN, 2)
+                    return carry
+
+                lax.fori_loop(step, octs, below_up, 0)
 
             @pl.when(jnp.logical_and(has_u, even_now))
             def _():
                 scale(xbuf, xs, first, down, oct_rows)
+
+                @pl.when(b == octs)
+                def _():
+                    gram(xs, first, 0, oct_rows, ybuf, first, 0, rows, XG, 1)
+                    gram(xs, first, oct_rows, rows - oct_rows, ybuf, first, rows - oct_rows, oct_rows, XG, 1)
 
                 def cross(j, carry):
                     gram(xs, first, down, oct_rows, ybuf, first, pl.multiple_of(j * oct_rows, oct_rows), oct_rows, XG, 1)
                     gram(xs, first, pl.multiple_of((octs - 1 - j) * oct_rows, oct_rows), oct_rows, ybuf, first, up, oct_rows, XG, 1)
                     return carry
 
-                lax.fori_loop(0, b, cross, 0)
+                lax.fori_loop(0, jnp.where(b == octs, 0, b), cross, 0)
 
             @pl.when(has_d)
             def _():
                 to_upper(step).wait_recv()
                 scale(ybuf, ys, second, down, oct_rows)
-                gram(ys, first, down, oct_rows, own, second, 0, rows, DG, 2)
+
+                def up_to_down(i, carry):
+                    gram(ys, first, down, oct_rows, own, second, pl.multiple_of(i * oct_rows, oct_rows), oct_rows, DG, 2)
+                    return carry
+
+                lax.fori_loop(0, octs - step, up_to_down, 0)
 
             @pl.when(jnp.logical_and(has_d, odd_now))
             def _():
+                @pl.when(b == octs)
+                def _():
+                    gram(ys, first, 0, oct_rows, xbuf, first, 0, rows, DG, 1)
+                    gram(ys, first, oct_rows, rows - oct_rows, xbuf, first, 0, oct_rows, DG, 1)
+
                 def cross(j, carry):
                     there = pl.multiple_of((octs - 1 - j) * oct_rows, oct_rows)
                     gram(ys, first, down, oct_rows, xbuf, first, there, oct_rows, DG, 1)
                     gram(ys, first, there, oct_rows, xbuf, first, down, oct_rows, DG, 1)
                     return carry
 
-                lax.fori_loop(0, b, cross, 0)
+                lax.fori_loop(0, jnp.where(b == octs, 0, b), cross, 0)
 
         each(send, LEAVE, b)
         each(hold, STAY, b)
@@ -457,6 +545,7 @@
         return carry
 
     lax.fori_loop(0, octs + 1, batch, 0)
+    walk(hand_on, passing, octs)
 
     def drain(b, carry):
         each(sent, LEAVE, b)
@@ -475,6 +564,8 @@
     def settle(slot, target):
         def step(o, carry):
             here = valid(slot, o, p)
+            if slot == XG:
+                here = jnp.logical_and(here, jnp.logical_not(is_late(given, o)))
 
             @pl.when(here)
             def _():
@@ -497,6 +588,18 @@
 
         lax.fori_loop(0, octs, step, 0)
 
+    def settle_direct(o, carry):
+        @pl.when(is_late(got, o))
+        def _():
+            value = total[OWN, rows_of(o), :] + relay[z, rows_of(o), :].astype(f32)
+            for hop in range(1, nz):
+                source = lax.rem(z + hop, nz)
+                onward(o, z, source).wait_recv()
+                value = value + direct[source, rows_of(o), :].astype(f32)
+            total[OWN, rows_of(o), :] = value
+
+        return carry
+
     settle(XG, mate)
     settle(DG, f - 2)
     settle(OWN, None)
@@ -516,7 +619,8 @@
 
     def from_mate(o):
         t = o + p
-        return jnp.logical_and(mate_gives, jnp.logical_and(t >= octs - 1, t <= 2 * octs - 1))
+        here = jnp.logical_and(mate_gives, jnp.logical_and(t >= octs - 1, t <= 2 * octs - 1))
+        return jnp.logical_and(here, jnp.logical_not(is_late(got, o)))
 
     def from_upper(o):
         t = o + p
@@ -525,6 +629,7 @@
 
     take(XG, mate, from_mate)
     take(DG, f - 2, from_upper)
+    lax.fori_loop(0, octs, settle_direct, 0)
 
     fin[...] = total[OWN]
     eye = lax.broadcasted_iota(jnp.int32, (freqs, freqs), 0) == lax.broadcasted_iota(
@@ -555,6 +660,7 @@
             out_ref[:, start:start + LANES] = jnp.where(live, values[k] * norm, 0.0)
 
     drain(octs, 0)
+    walk(handed, passing, octs)
 
     def close(o, carry):
         to_mate(o).wait_send()
@@ -567,7 +673,7 @@
         def _():
             to_upper(o).wait_send()
 
-        @pl.when(valid(XG, o, p))
+        @pl.when(jnp.logical_and(valid(XG, o, p), jnp.logical_not(is_late(given, o))))
         def _():
             forward(XG, mate, o).wait_send()
 
@@ -612,6 +718,8 @@
             pltpu.VMEM((3, rows, LANES), bf16),
             pltpu.VMEM((3, rows, LANES), bf16),
             pltpu.VMEM((rows, LANES), f32),
+            pltpu.VMEM((nz, rows, LANES), bf16),
+            pltpu.VMEM((nz, rows, LANES), bf16),
             pltpu.VMEM((1, panels), jnp.int32),
             pltpu.VMEM((1, freqs), jnp.int32),
             pltpu.SemaphoreType.REGULAR((2, max(nz - 2, 1))),
@@ -620,6 +728,7 @@
             dma((3, nz, octs)), dma((3, nz, octs)),
             dma((3, nz, octs)), dma((3, nz, octs)),
             dma((3, octs)), dma((3, octs)),
+            dma((nz, octs)), dma((nz, octs)), dma((nz, octs)),
         ],
         compiler_params=pltpu.CompilerParams(
             collective_id=0, has_side_effects=True, vmem_limit_bytes=58 * 1024 * 1024

time: 47.4 us -> 46.5 us (0.981)
  Pallas kernels: 45.5 us -> 44.7 us
    pallas_call x1, Pallas kernels: 45.5 us -> 44.7 us  [fused(): pl.pallas_call(functools.partial(kernel, nf, npan), out_shape=jax.ShapeDt...]
where the time goes in v4:
time: 46.5 us; the launch traced here: 46.3 us
  Pallas kernels  44.7 us (96%)
  local copies, waits for them, and re-layouts  1.67 us (4%)
    pallas_call x1, Pallas kernels, fused(): pl.pallas_call(functools.partial(kernel, nf, npan), out_shape=jax.ShapeDt...  44.7 us
    unnamed x1, local copies, waits for them, and re-layouts  1.67 us

profile of v4, /device:TPU:0, one launch (start us, length us, event | category | flops | bytes accessed | tf_op | source)
XLA Modules:
  0.0 46.3 jit_solution(4194247203839704271)
XLA Ops:
  0.0 44.7 %shard_map.37 = f32[32,2048]{1,0:T(8,128)} custom-call(bf16[512,2048]{1,0:T(8,128)(2,1)} %bitcast.3, s32[1,2048]{1,0:T(1,128)} %bitcast.4, s32[1,32]{1,0:T(1,128)} %bitcast.5), custom_call_target="tpu_custom_call" | custom-call | tf_op jit(solution)/shard_map/pallas_call | solution.py:699
  44.7 1.7 %copy.5 = f32[32,2048]{1,0:T(8,128)} copy(f32[32,2048]{1,0:T(8,128)} %shard_map.37) | data formatting | bytes 524288

commit v5 on v4

--- a/solution.py
+++ b/solution.py
@@ -107,14 +107,13 @@
 
 
 def kernel(
-    nf, npan, f_hbm, q_hbm, bw_hbm, out_ref,
-    own, scaled, xbuf, ybuf, xs, ys, acc, keep, away, cxin, zout, zin, total, give, fwd, fin, relay, direct,
-    q_ref, bw_ref, near, local_sem, fsend, frecv, csend, crecv, zsend, zrecv, gsend, grecv, rsend, rrecv, drecv,
+    nf, npan, f_hbm, q_hbm, out_ref,
+    own, scaled, xbuf, ybuf, xs, ys, acc, keep, away, cxin, zout, zin, total, give, fwd, relay, direct,
+    q_ref, near, local_sem, fsend, frecv, csend, crecv, zsend, zrecv, gsend, grecv, rsend, rrecv, drecv,
 ):
     rows, panels = own.shape
     half = panels // 2
     block = rows
-    freqs = rows // COMP
     oct_rows = 8 * COMP
     octs = rows // oct_rows
     nz = npan // CORES
@@ -162,7 +161,6 @@
     loads = [
         pltpu.make_async_copy(f_hbm, own, local_sem.at[0]),
         pltpu.make_async_copy(q_hbm, q_ref, local_sem.at[1]),
-        pltpu.make_async_copy(bw_hbm, bw_ref, local_sem.at[2]),
     ]
     for load in loads:
         load.start()
@@ -232,14 +230,18 @@
                 value = jnp.where(seat == role * CORES + side, jnp.int32(of(role, side)), value)
         return value
 
+    def group(role, side, b, own_tiles):
+        return [tile for tile in plans[role][0][side][b] if (tile[0] == OWN) == own_tiles]
+
     orders = []
     for seat in (f * CORES + 1 - core, f * CORES + core):
-        orders.append([
-            [mine(seat, lambda role, side: len(plans[role][0][side][b]))]
-            + [mine(seat, lambda role, side: packed(plans[role][0][side][b], w)) for w in range(words)]
-            for b in range(octs + 1)
-        ])
-    LEAVE, STAY = orders
+        for kind in (False, True):
+            orders.append([
+                [mine(seat, lambda role, side: len(group(role, side, b, kind)))]
+                + [mine(seat, lambda role, side: packed(group(role, side, b, kind), w)) for w in range(words)]
+                for b in range(octs + 1)
+            ])
+    LEAVE_CROSS, LEAVE_OWN, STAY_CROSS, STAY_OWN = orders
     busy = jnp.logical_or(jnp.logical_and(has_u, odd == 0), jnp.logical_and(has_d, odd == 1))
 
     def crossing(role, side):
@@ -471,11 +473,12 @@
     gram(scaled, everything, 0, rows, own, everything, 0, rows, OWN, 0)
 
     def batch(b, carry):
+        step = jnp.maximum(b - 1, 0)
+        down = pl.multiple_of((octs - 1 - step) * oct_rows, oct_rows)
+        up = pl.multiple_of(step * oct_rows, oct_rows)
+
         @pl.when(b > 0)
         def _():
-            step = b - 1
-            down = pl.multiple_of((octs - 1 - step) * oct_rows, oct_rows)
-            up = pl.multiple_of(step * oct_rows, oct_rows)
             to_mate(step).wait_recv()
 
             @pl.when(odd_now)
@@ -483,19 +486,9 @@
                 scale(xbuf, xs, second, down, oct_rows)
                 gram(xs, first, down, oct_rows, own, second, 0, rows, XG, 1)
 
-            @pl.when(even_now)
-            def _():
-                gram(scaled, first, 0, rows, xbuf, first, down, oct_rows, OWN, 1)
-
             @pl.when(has_u)
             def _():
                 to_lower(step).wait_recv()
-
-                def below_up(i, carry):
-                    gram(scaled, first, pl.multiple_of(i * oct_rows, oct_rows), oct_rows, ybuf, first, up, oct_rows, OWN, 2)
-                    return carry
-
-                lax.fori_loop(step, octs, below_up, 0)
 
             @pl.when(jnp.logical_and(has_u, even_now))
             def _():
@@ -507,8 +500,9 @@
                     gram(xs, first, oct_rows, rows - oct_rows, ybuf, first, rows - oct_rows, oct_rows, XG, 1)
 
                 def cross(j, carry):
+                    there = pl.multiple_of((octs - 1 - j) * oct_rows, oct_rows)
                     gram(xs, first, down, oct_rows, ybuf, first, pl.multiple_of(j * oct_rows, oct_rows), oct_rows, XG, 1)
-                    gram(xs, first, pl.multiple_of((octs - 1 - j) * oct_rows, oct_rows), oct_rows, ybuf, first, up, oct_rows, XG, 1)
+                    gram(xs, first, there, oct_rows, ybuf, first, up, oct_rows, XG, 1)
                     return carry
 
                 lax.fori_loop(0, jnp.where(b == octs, 0, b), cross, 0)
@@ -539,17 +533,37 @@
 
                 lax.fori_loop(0, jnp.where(b == octs, 0, b), cross, 0)
 
-        each(send, LEAVE, b)
-        each(hold, STAY, b)
-        each(join, STAY, b)
+        each(send, LEAVE_CROSS, b)
+
+        @pl.when(b > 0)
+        def _():
+            @pl.when(even_now)
+            def _():
+                gram(scaled, first, 0, rows, xbuf, first, down, oct_rows, OWN, 1)
+
+            @pl.when(has_u)
+            def _():
+                def below_up(i, carry):
+                    gram(scaled, first, pl.multiple_of(i * oct_rows, oct_rows), oct_rows, ybuf, first, up, oct_rows, OWN, 2)
+                    return carry
+
+                lax.fori_loop(step, octs, below_up, 0)
+
+        each(send, LEAVE_OWN, b)
+        each(hold, STAY_CROSS, b)
+        each(join, STAY_CROSS, b)
+        each(hold, STAY_OWN, b)
+        each(join, STAY_OWN, b)
         return carry
 
     lax.fori_loop(0, octs + 1, batch, 0)
     walk(hand_on, passing, octs)
 
     def drain(b, carry):
-        each(sent, LEAVE, b)
-        each(joined, STAY, b)
+        for order in (LEAVE_CROSS, LEAVE_OWN):
+            each(sent, order, b)
+        for order in (STAY_CROSS, STAY_OWN):
+            each(joined, order, b)
         return carry
 
     lax.fori_loop(0, octs, drain, 0)
@@ -631,7 +645,39 @@
     take(DG, f - 2, from_upper)
     lax.fori_loop(0, octs, settle_direct, 0)
 
-    fin[...] = total[OWN]
+    out_ref[...] = total[OWN]
+
+    drain(octs, 0)
+    walk(handed, passing, octs)
+
+    def close(o, carry):
+        to_mate(o).wait_send()
+
+        @pl.when(has_d)
+        def _():
+            to_lower(o).wait_send()
+
+        @pl.when(has_u)
+        def _():
+            to_upper(o).wait_send()
+
+        @pl.when(jnp.logical_and(valid(XG, o, p), jnp.logical_not(is_late(given, o))))
+        def _():
+            forward(XG, mate, o).wait_send()
+
+        @pl.when(valid(DG, o, p))
+        def _():
+            forward(DG, f - 2, o).wait_send()
+
+        return carry
+
+    lax.fori_loop(0, octs, close, 0)
+
+
+def finalize(panels_total, bw_ref, sum_ref, blocks_ref):
+    f32 = jnp.float32
+    freqs = blocks_ref.shape[0]
+    p = lax.axis_index("panel")
     eye = lax.broadcasted_iota(jnp.int32, (freqs, freqs), 0) == lax.broadcasted_iota(
         jnp.int32, (freqs, freqs), 1
     )
@@ -639,10 +685,10 @@
         jnp.where(eye, jnp.broadcast_to(bw_ref[...].astype(f32), (freqs, freqs)), 0.0), 1, keepdims=True
     )
     width = jnp.broadcast_to(width, (freqs, LANES))
-    norm = jnp.float32(1.0 / math.sqrt(panels * npan))
+    norm = jnp.float32(1.0 / math.sqrt(panels_total))
     part = lax.broadcasted_iota(jnp.int32, (freqs, LANES), 1) // COMP
     for h in range(COMP // 8):
-        values = [fin[pl.ds(h * 8 + a, freqs, stride=COMP), :] for a in range(8)]
+        values = [sum_ref[pl.ds(h * 8 + a, freqs, stride=COMP), :] for a in range(8)]
         for bit in (1, 2, 4):
             upper = lax.rem(part // bit, 2) == 1
             fresh = list(values)
@@ -657,33 +703,7 @@
             offset = (p * 8 + k + 1).astype(f32)
             live = offset <= width
             start = (k * (COMP // 8) + h) * LANES
-            out_ref[:, start:start + LANES] = jnp.where(live, values[k] * norm, 0.0)
-
-    drain(octs, 0)
-    walk(handed, passing, octs)
-
-    def close(o, carry):
-        to_mate(o).wait_send()
-
-        @pl.when(has_d)
-        def _():
-            to_lower(o).wait_send()
-
-        @pl.when(has_u)
-        def _():
-            to_upper(o).wait_send()
-
-        @pl.when(jnp.logical_and(valid(XG, o, p), jnp.logical_not(is_late(given, o))))
-        def _():
-            forward(XG, mate, o).wait_send()
-
-        @pl.when(valid(DG, o, p))
-        def _():
-            forward(DG, f - 2, o).wait_send()
-
-        return carry
-
-    lax.fori_loop(0, octs, close, 0)
+            blocks_ref[:, start:start + LANES] = jnp.where(live, values[k] * norm, 0.0)
 
 
 def fused(nf, npan, fields, quad_index, band_width):
@@ -696,10 +716,10 @@
     bf16, f32 = jnp.bfloat16, jnp.float32
     dma = pltpu.SemaphoreType.DMA
     vmem = pl.BlockSpec(memory_space=pltpu.VMEM)
-    return pl.pallas_call(
+    sums = pl.pallas_call(
         functools.partial(kernel, nf, npan),
-        out_shape=jax.ShapeDtypeStruct((freqs, out_cols), f32),
-        in_specs=[pl.BlockSpec(memory_space=pl.ANY)] * 3,
+        out_shape=jax.ShapeDtypeStruct((rows, LANES), f32),
+        in_specs=[pl.BlockSpec(memory_space=pltpu.HBM)] * 2,
         out_specs=vmem,
         scratch_shapes=[
             pltpu.VMEM((rows, panels), bf16),
@@ -717,13 +737,11 @@
             pltpu.VMEM((3, rows, LANES), f32),
             pltpu.VMEM((3, rows, LANES), bf16),
             pltpu.VMEM((3, rows, LANES), bf16),
-            pltpu.VMEM((rows, LANES), f32),
             pltpu.VMEM((nz, rows, LANES), bf16),
             pltpu.VMEM((nz, rows, LANES), bf16),
             pltpu.VMEM((1, panels), jnp.int32),
-            pltpu.VMEM((1, freqs), jnp.int32),
             pltpu.SemaphoreType.REGULAR((2, max(nz - 2, 1))),
-            dma((3,)),
+            dma((2,)),
             dma((2, octs)), dma((2, octs)),
             dma((3, nz, octs)), dma((3, nz, octs)),
             dma((3, nz, octs)), dma((3, nz, octs)),
@@ -731,9 +749,19 @@
             dma((nz, octs)), dma((nz, octs)), dma((nz, octs)),
         ],
         compiler_params=pltpu.CompilerParams(
-            collective_id=0, has_side_effects=True, vmem_limit_bytes=58 * 1024 * 1024
+            collective_id=0, has_side_effects=True, vmem_limit_bytes=40 * 1024 * 1024
         ),
-    )(fields.reshape(rows, panels), quad_index.reshape(1, panels), band_width.reshape(1, freqs))
+    )(
+        pltpu.with_memory_space_constraint(fields.reshape(rows, panels), pltpu.HBM),
+        pltpu.with_memory_space_constraint(quad_index.reshape(1, panels), pltpu.HBM),
+    )
+    return pl.pallas_call(
+        functools.partial(finalize, panels * npan),
+        out_shape=jax.ShapeDtypeStruct((freqs, out_cols), f32),
+        in_specs=[vmem, vmem],
+        out_specs=vmem,
+        compiler_params=pltpu.CompilerParams(vmem_limit_bytes=8 * 1024 * 1024),
+    )(band_width.reshape(1, freqs), sums)
 
 
 def local(nf, npan, fields, quad_index, band_width):

time: 46.5 us -> 44.4 us (0.955)
  local copies, waits for them, and re-layouts: 1.67 us -> 0.01 us
  Pallas kernels: 44.7 us -> 44.2 us
    unnamed x1 -> x2, local copies, waits for them, and re-layouts: 1.67 us -> 0.01 us
    pallas_call x1, Pallas kernels: 44.7 us -> 43.1 us  [fused(): pl.pallas_call(functools.partial(kernel, nf, npan), out_shape=jax.ShapeDt...]
    pallas_call x0 -> x1, Pallas kernels: none -> 1.14 us  [fused(): pl.pallas_call(functools.partial(finalize, panels * npan), out_shape=jax....]
where the time goes in v5:
time: 44.4 us; the launch traced here: 44.2 us
  Pallas kernels  44.2 us (100%)
    pallas_call x1, Pallas kernels, fused(): pl.pallas_call(functools.partial(kernel, nf, npan), out_shape=jax.ShapeDt...  43.1 us
    pallas_call x1, Pallas kernels, fused(): pl.pallas_call(functools.partial(finalize, panels * npan), out_shape=jax....  1.14 us

profile of v5, /device:TPU:0, one launch (start us, length us, event | category | flops | bytes accessed | tf_op | source)
XLA Modules:
  0.0 44.2 jit_solution(879507208937012789)
XLA Ops:
  0.0 0.0 copy-start
  0.0 43.1 %shard_map.37.sum_ref = f32[512,128]{1,0:T(8,128)S(1)} custom-call(bf16[512,2048]{1,0:T(8,128)(2,1)} %bitcast.4, s32[1,2048]{1,0:T(1,128)} %bitcast.5), custom_call_target="tpu_custom_call" | custom-call | tf_op jit(solution)/shard_map/pallas_call | solution.py:719
  43.1 0.0 copy-done
  43.1 1.1 %shard_map.38 = f32[32,2048]{1,0:T(8,128)} custom-call(s32[1,32]{1,0:T(1,128)S(1)} %bitcast.3, f32[512,128]{1,0:T(8,128)S(1)} %shard_map.37.sum_ref), custom_call_target="tpu_custom_call" | custom-call | tf_op jit(solution)/shard_map/pallas_call | solution.py:758
Async XLA Ops:
  0.0 43.1 %copy-start = (s32[32]{0:T(128)S(1)}, s32[32]{0:T(128)}, u32[]{:S(2)}) copy-start(s32[32]{0:T(128)} %param.5) | copy-start | bytes 388

commit v6 on v5

--- a/solution.py
+++ b/solution.py
@@ -162,9 +162,6 @@
         pltpu.make_async_copy(f_hbm, own, local_sem.at[0]),
         pltpu.make_async_copy(q_hbm, q_ref, local_sem.at[1]),
     ]
-    for load in loads:
-        load.start()
-
     count = 2
     for there in (below, above, has_u, has_d):
         count = count + jnp.where(there, 1, 0)
@@ -206,6 +203,8 @@
         return carry
 
     lax.fori_loop(0, octs, depart, 0)
+    for load in loads:
+        load.start()
 
     plans = [plan(role, octs, npan) for role in range(nf)]
     base = 1

time: 44.4 us -> 44.4 us (level)
  no operation moved by 1% of the time
where the time goes in v6:
time: 44.4 us; the launch traced here: 44.2 us
  Pallas kernels  44.2 us (100%)
    pallas_call x1, Pallas kernels, fused(): pl.pallas_call(functools.partial(kernel, nf, npan), out_shape=jax.ShapeDt...  43.1 us
    pallas_call x1, Pallas kernels, fused(): pl.pallas_call(functools.partial(finalize, panels * npan), out_shape=jax....  1.14 us

profile of v6, /device:TPU:0, one launch (start us, length us, event | category | flops | bytes accessed | tf_op | source)
XLA Modules:
  0.0 44.2 jit_solution(1184361763276166515)
XLA Ops:
  0.0 0.0 copy-start
  0.0 43.1 %shard_map.37.sum_ref = f32[512,128]{1,0:T(8,128)S(1)} custom-call(bf16[512,2048]{1,0:T(8,128)(2,1)} %bitcast.4, s32[1,2048]{1,0:T(1,128)} %bitcast.5), custom_call_target="tpu_custom_call" | custom-call | tf_op jit(solution)/shard_map/pallas_call | solution.py:718
  43.1 0.0 copy-done
  43.1 1.1 %shard_map.38 = f32[32,2048]{1,0:T(8,128)} custom-call(s32[1,32]{1,0:T(1,128)S(1)} %bitcast.3, f32[512,128]{1,0:T(8,128)S(1)} %shard_map.37.sum_ref), custom_call_target="tpu_custom_call" | custom-call | tf_op jit(solution)/shard_map/pallas_call | solution.py:757
Async XLA Ops:
  0.0 43.1 %copy-start = (s32[32]{0:T(128)S(1)}, s32[32]{0:T(128)}, u32[]{:S(2)}) copy-start(s32[32]{0:T(128)} %param.5) | copy-start | bytes 388
